TPU v7x, 128 devices: a whole 4x4x4 slice. The times are simulated.
128 devices in a mesh: cp: 4 (over y), ep: 32 (over x, z, core).
Axes of the slice: x: 4, y: 4, z: 4, core: 2. Of those that a mesh axis runs over, the one named last changes fastest.
Arguments:
- tokens: bfloat16 [32, 256, 3584], P('ep', 'cp'), may hold values from -6 to 6
- cotangent: bfloat16 [32, 256, 3584], P('ep', 'cp'), may hold values from -6 to 6
- routes: int32 [32, 256, 8], P('ep', 'cp'), may hold values from 0 to 127, all different within a row; in each aligned block of 64 rows (0 to 63, 64 to 127, ..., all dimensions but the last counted through in order) at most 5 rows name the same one
- router_weights: float32 [32, 256, 8], P('ep', 'cp'), may hold values from 0.02 to 0.5
- w_gate: bfloat16 [128, 3584, 1024], P(('cp', 'ep')), may hold values from -0.09375 to 0.09375
- w_up: bfloat16 [128, 3584, 1024], P(('cp', 'ep')), may hold values from -0.09375 to 0.09375
- w_down: bfloat16 [128, 1024, 3584], P(('cp', 'ep')), may hold values from -0.1875 to 0.1875
Outputs:
- layer_out: bfloat16 [32, 256, 3584], P('ep', 'cp')
- token_grad: bfloat16 [32, 256, 3584], P('ep', 'cp')
- gate_grad: float32 [32, 256, 8], P('ep', 'cp')
Inputs may be any that keep to these rules, and one draw needn't show every extreme that they name: `routes`: each row names 8 distinct experts; in each aligned block of 64 rows (the rows of one device) no expert is named by more than 5 of the block's slots.
All inputs are finite; a program needn't handle non-finite values.
Results may differ from a plain program's by a relative error of at most 0.0058.
Values may be sent and summed in bfloat16 or wider, within the bound.
No kernel may reach another device: no remote copies, remote signals or barrier semaphores. Data moves between devices by JAX's collectives and lax.ppermute only.
A program may use at most 128 MiB of HBM per device.

v0:
```python
import jax
import jax.numpy as jnp
from jax import lax
from jax.sharding import PartitionSpec as P


def exchange_in_groups(value, axis, split_dim, concat_dim, work, item_dim, out_dim):
    items = jax.tree.leaves(value)[0].shape[item_dim]
    count = 4 if items % 4 == 0 else 1
    gathered = []
    for k in range(count):
        group = jax.tree.map(
            lambda a: lax.slice_in_dim(
                a, k * (items // count), (k + 1) * (items // count), axis=item_dim
            ),
            value,
        )
        gathered.append(
            work(
                lax.all_to_all(
                    group, axis, split_axis=split_dim, concat_axis=concat_dim, tiled=True
                )
            )
        )
    return jax.tree.map(lambda *parts: jnp.concatenate(parts, axis=out_dim), *gathered)


def expert_rows(stacked, gate_matrix, up_matrix, down_matrix):
    inputs = stacked[:, 0]
    grad_in = stacked[:, 1]
    gate_pre = jnp.dot(inputs, gate_matrix, preferred_element_type=jnp.float32)
    up_pre = jnp.dot(inputs, up_matrix, preferred_element_type=jnp.float32)
    sig_gate = jax.nn.sigmoid(gate_pre)
    silu_gate = gate_pre * sig_gate
    hidden = (silu_gate * up_pre).astype(jnp.bfloat16)
    expert_out = jnp.dot(hidden, down_matrix, preferred_element_type=jnp.float32).astype(
        jnp.bfloat16
    )
    grad_hidden = jnp.dot(grad_in, down_matrix.T, preferred_element_type=jnp.float32)
    grad_gate = (grad_hidden * up_pre * sig_gate * (1.0 + gate_pre * (1.0 - sig_gate))).astype(
        jnp.bfloat16
    )
    grad_up = (grad_hidden * silu_gate).astype(jnp.bfloat16)
    expert_grad = (
        jnp.dot(grad_gate, gate_matrix.T, preferred_element_type=jnp.float32)
        + jnp.dot(grad_up, up_matrix.T, preferred_element_type=jnp.float32)
    ).astype(jnp.bfloat16)
    return jnp.stack([expert_out, expert_grad], 1)


def per_device(tokens, cotangent, routes, router_weights, w_gate, w_up, w_down):
    cp_count = lax.axis_size("cp")
    ep_count = lax.axis_size("ep")
    owners = cp_count * ep_count
    positions = tokens.shape[1]
    features = tokens.shape[2]
    top_k = routes.shape[2]
    capacity = positions * top_k // owners * 5 // 4
    gate_matrix = w_gate[0]
    up_matrix = w_up[0]
    down_matrix = w_down[0]
    flat_routes = routes[0].reshape(positions * top_k)
    one_hot = (flat_routes[:, None] == jnp.arange(owners, dtype=jnp.int32)[None, :]).astype(
        jnp.int32
    )
    before = jnp.cumsum(one_hot, axis=0) - one_hot
    ranking = jnp.sum(before * one_hot, axis=1)
    dest_slot = flat_routes * capacity + ranking
    token_of = jnp.arange(positions * top_k, dtype=jnp.int32) // top_k
    slot_token = jnp.full((owners * capacity,), positions, jnp.int32).at[dest_slot].set(token_of)
    stacked = jnp.concatenate(
        [jnp.stack([tokens[0], cotangent[0]], 1), jnp.zeros((1, 2, features), jnp.bfloat16)], 0
    )
    send_rows = stacked[slot_token]

    def serve_rows(received):
        outcome = expert_rows(
            received.reshape(-1, 2, features), gate_matrix, up_matrix, down_matrix
        )
        return lax.all_to_all(
            outcome.reshape(received.shape), ("cp", "ep"), split_axis=0, concat_axis=0, tiled=True
        )

    returned = exchange_in_groups(
        send_rows.reshape(owners, capacity, 2, features), ("cp", "ep"), 0, 0, serve_rows, 1, 1
    )
    fetched = returned.reshape(owners * capacity, 2, features)[dest_slot]
    expert_out = fetched[:, 0].reshape(positions, top_k, features).astype(jnp.float32)
    expert_grad = fetched[:, 1].reshape(positions, top_k, features).astype(jnp.float32)
    mixing = router_weights[0]
    layer_out = jnp.einsum("tk,tkd->td", mixing, expert_out)
    token_grad = jnp.einsum("tk,tkd->td", mixing, expert_grad)
    gate_grad = jnp.sum(cotangent[0].astype(jnp.float32)[:, None, :] * expert_out, axis=-1)
    return (
        layer_out.astype(jnp.bfloat16)[None],
        token_grad.astype(jnp.bfloat16)[None],
        gate_grad[None],
    )


def solution(mesh):
    in_specs = (
        P("ep", "cp", None),
        P("ep", "cp", None),
        P("ep", "cp", None),
        P("ep", "cp", None),
        P(("cp", "ep"), None, None),
        P(("cp", "ep"), None, None),
        P(("cp", "ep"), None, None),
    )
    out_specs = (P("ep", "cp", None), P("ep", "cp", None), P("ep", "cp", None))
    return jax.shard_map(
        per_device, mesh=mesh, in_specs=in_specs, out_specs=out_specs, check_vma=False
    )
```

profile of v0, /device:TPU:34, one launch (start us, length us, event | category | flops | bytes accessed | tf_op | source)
XLA Modules:
  0.0 482.0 jit_solution(17294831272711744417)
XLA Ops:
  0.6 0.8 copy.29
  1.6 0.7 broadcast_multiply_fusion
  2.4 0.2 fusion.40
  2.9 0.2 fusion.39
  3.1 2.4 scatter_custom_fusion
  5.6 1.7 copy.26
  7.3 1.7 copy.27
  9.1 2.1 fusion.33
  11.2 31.5 %gather_fusion = bf16[640,2,3584]{2,1,0:T(2,128)(2,1)} fusion(bf16[65,2,3584]{2,1,0:T(2,128)(2,1)S(1)} %fusion.33, s32[1024]{0:T(1024)S(1)} %pad_clamp_fusion.1), kind=kCustom, calls=%fused_computation | custom fusion | bytes 18352640 | tf_op jit(solution)/shard_map/gather | solution.py:74
  42.7 115.1 %all_to_all.10 = bf16[128,5,2,3584]{3,2,1,0:T(2,128)(2,1)S(1)} all-to-all(bf16[128,5,2,3584]{3,2,1,0:T(2,128)(2,1)} %bitcast.73), channel_id=1, replica_groups=mesh['cp'=4,'ep'=32] {'cp','ep'}, dimensions={0} | all-to-all | bytes 18350080 | tf_op jit(solution)/shard_map/all_to_all | solution.py:20
  157.8 13.7 %fusion.51 = (bf16[640,1,3584]{2,1,0:T(2,128)(2,1)}, bf16[640,1,3584]{2,1,0:T(2,128)(2,1)S(1)}) fusion(bf16[640,2,3584]{2,1,0:T(2,128)(2,1)S(1)} %bitcast.72), kind=kLoop, calls=%fused_computation.73 | loop fusion | bytes 18350080 | tf_op jit(solution)/shard_map/slice | solution.py:29
  171.5 9.8 %fusion.10 = f32[640,1024]{1,0:T(8,128)S(1)} fusion(bf16[1,3584,1024]{2,1,0:T(8,128)(2,1)} %param.11, bf16[640,1,3584]{2,1,0:T(2,128)(2,1)} %get-tuple-element.12), kind=kOutput, calls=%fused_computation.15 | convolution fusion | flops 4697620480 | bytes 14548992 | tf_op jit(solution)/shard_map/dot_general | solution.py:31
  181.3 9.6 %fusion.6 = f32[640,1024]{1,0:T(8,128)} fusion(bf16[1,3584,1024]{2,1,0:T(8,128)(2,1)} %param.12, bf16[640,1,3584]{2,1,0:T(2,128)(2,1)S(1)} %copy-done.1), kind=kOutput, calls=%fused_computation.11 | convolution fusion | flops 4697620480 | bytes 14548992 | tf_op jit(solution)/shard_map/dot_general | solution.py:32
  190.9 8.7 %fusion = f32[640,1024]{1,0:T(8,128)} fusion(bf16[1,1024,3584]{2,1,0:T(8,128)(2,1)} %param.13, bf16[640,1,3584]{2,1,0:T(2,128)(2,1)S(1)} %get-tuple-element.13), kind=kOutput, calls=%fused_computation.5 | convolution fusion | flops 4697620480 | bytes 14548992 | tf_op jit(solution)/shard_map/dot_general | solution.py:39
  199.6 12.5 %fusion.4 = f32[640,3584]{1,0:T(8,128)} fusion(bf16[1,3584,1024]{2,1,0:T(8,128)(2,1)} %param.12, f32[640,1024]{1,0:T(8,128)} %fusion, f32[640,1024]{1,0:T(8,128)S(1)} %fusion.10), kind=kOutput, calls=%fused_computation.9 | convolution fusion | flops 4701552640 | bytes 21757952 | tf_op jit(solution)/shard_map/dot_general | solution.py:46
  212.2 9.9 %fusion.12 = bf16[640,3584]{1,0:T(8,128)(2,1)} fusion(bf16[1,1024,3584]{2,1,0:T(8,128)(2,1)} %param.13, f32[640,1024]{1,0:T(8,128)S(1)} %copy-done.5, f32[640,1024]{1,0:T(8,128)S(1)} %fusion.10), kind=kOutput, calls=%fused_computation.18 | convolution fusion | flops 4703846400 | bytes 17170432 | tf_op jit(solution)/shard_map/dot_general | solution.py:36
  222.1 15.8 %add_convert_fusion = bf16[640,3584]{1,0:T(8,128)(2,1)} fusion(f32[640,3584]{1,0:T(8,128)} %fusion.4, bf16[1,3584,1024]{2,1,0:T(8,128)(2,1)} %param.11, f32[640,1024]{1,0:T(8,128)} %copy-done.4, f32[640,1024]{1,0:T(8,128)} %fusion, f32[640,1024]{1,0:T(8,128)} %fusion.6), kind=kOutput, calls=%fused_computation.4 | convolution fusion | flops 4708761600 | bytes 28966912 | tf_op jit(solution)/shard_map/dot_general | solution.py:45
  237.9 7.8 %stack.14 = bf16[128,5,1,3584]{3,1,0,2:T(8,128)(2,1)} reshape(bf16[640,3584]{1,0:T(8,128)(2,1)} %add_convert_fusion) | data formatting | bytes 9175040 | tf_op jit(solution)/shard_map/stack | solution.py:48
  245.8 7.8 %stack.13 = bf16[128,5,1,3584]{3,1,0,2:T(8,128)(2,1)} reshape(bf16[640,3584]{1,0:T(8,128)(2,1)} %fusion.12) | data formatting | bytes 9175040 | tf_op jit(solution)/shard_map/stack | solution.py:48
  253.6 8.6 %pad_maximum_fusion = bf16[128,5,2,3584]{3,1,0,2:T(8,128)(2,1)S(1)} fusion(bf16[128,5,1,3584]{3,1,0,2:T(8,128)(2,1)} %stack.14, bf16[128,5,1,3584]{3,1,0,2:T(8,128)(2,1)} %stack.13), kind=kLoop, calls=%fused_computation.3 | loop fusion | flops 4587520 | bytes 18350080 | tf_op jit(solution)/shard_map/stack | solution.py:48
  262.2 9.8 %copy.33 = bf16[128,5,2,3584]{3,2,1,0:T(2,128)(2,1)} copy(bf16[128,5,2,3584]{3,1,0,2:T(8,128)(2,1)S(1)} %pad_maximum_fusion) | data formatting | bytes 18350080 | tf_op jit(solution)/shard_map/stack | solution.py:48
  272.0 11.7 %all-to-all-start.1 = ((bf16[128,5,2,3584]{3,2,1,0:T(2,128)(2,1)}), bf16[128,5,2,3584]{3,2,1,0:T(2,128)(2,1)}, u32[]{:S(2)}, u32[]{:S(2)}) async-start(bf16[128,5,2,3584]{3,2,1,0:T(2,128)(2,1)} %copy.33), calls=%async_computation.1 | async-start | bytes 18350080 | tf_op jit(solution)/shard_map/all_to_all | solution.py:80
  283.9 3.8 mul.62
  287.7 11.7 %mul.63 = f32[512,1,3584]{2,1,0:T(1,128)} reshape(f32[64,8,3584]{2,1,0:T(8,128)} %mul.62) | data formatting | bytes 14680064 | tf_op jit(solution)/shard_map/mul | solution.py:93
  299.5 99.4 %all-to-all-done.1 = bf16[128,5,2,3584]{3,2,1,0:T(2,128)(2,1)} async-done(((bf16[128,5,2,3584]{3,2,1,0:T(2,128)(2,1)}), bf16[128,5,2,3584]{3,2,1,0:T(2,128)(2,1)}, u32[]{:S(2)}, u32[]{:S(2)}) %all-to-all-start.1) | async-done | bytes 9175072 | tf_op jit(solution)/shard_map/all_to_all | solution.py:80
  398.8 29.4 %gather_fusion.1 = bf16[512,2,3584]{2,1,0:T(2,128)(2,1)} fusion(bf16[640,2,3584]{2,1,0:T(2,128)(2,1)} %bitcast.12, s32[1024]{0:T(1024)S(1)} %pad_clamp_fusion), kind=kCustom, calls=%fused_computation.1 | custom fusion | bytes 14682112 | tf_op jit(solution)/shard_map/gather | solution.py:87
  428.3 15.3 %fusion.52 = (bf16[512,1,3584]{2,1,0:T(2,128)(2,1)}, bf16[512,1,3584]{2,1,0:T(2,128)(2,1)S(1)}) fusion(bf16[512,2,3584]{2,1,0:T(2,128)(2,1)} %gather_fusion.1), kind=kLoop, calls=%fused_computation.74 | loop fusion | bytes 14680064 | tf_op jit(solution)/shard_map/slice | solution.py:89
  443.5 5.3 %fusion.21 = bf16[64,1,3584]{2,1,0:T(2,128)(2,1)} fusion(bf16[64,8,1]{1,2,0:T(2,128)(2,1)S(1)} %copy.35, bf16[512,1,3584]{2,1,0:T(2,128)(2,1)} %get-tuple-element.14), kind=kOutput, calls=%fused_computation.23 | convolution fusion | flops 3670016 | bytes 4129792 | tf_op jit(solution)/shard_map/tk,tkd->td/dot_general | solution.py:92
  448.8 2.1 fusion.24
  450.9 27.7 %multiply_reduce_fusion = f32[512]{0:T(512)S(1)} fusion(f32[512,1,3584]{2,1,0:T(1,128)S(1)} %bitcast.75, bf16[512,2,3584]{2,1,0:T(2,128)(2,1)S(1)} %copy-done), kind=kLoop, calls=%fused_computation.17 | loop fusion | flops 5504512 | bytes 11012096 | tf_op jit(solution)/shard_map/reduce_sum | solution.py:93
  478.6 0.7 copy.34
  479.3 2.5 fusion.34
  (36 shorter events, 0.9 us)
Async XLA Ops:
  171.5 9.8 %copy-start.1 = (bf16[640,1,3584]{2,1,0:T(2,128)(2,1)S(1)}, bf16[640,1,3584]{2,1,0:T(2,128)(2,1)}, u32[]{:S(2)}) copy-start(bf16[640,1,3584]{2,1,0:T(2,128)(2,1)} %get-tuple-element.12) | copy-start | bytes 13762564
  181.3 30.9 %copy-start.4 = (f32[640,1024]{1,0:T(8,128)}, f32[640,1024]{1,0:T(8,128)S(1)}, u32[]{:S(2)}) copy-start(f32[640,1024]{1,0:T(8,128)S(1)} %fusion.10) | copy-start | bytes 7864324
  199.6 12.6 %copy-start.5 = (f32[640,1024]{1,0:T(8,128)S(1)}, f32[640,1024]{1,0:T(8,128)}, u32[]{:S(2)}) copy-start(f32[640,1024]{1,0:T(8,128)} %fusion.6) | copy-start | bytes 7864324
  272.0 11.7 %copy-start.3 = (f32[1,64,8]{1,2,0:T(8,128)S(1)}, f32[1,64,8]{1,2,0:T(8,128)}, u32[]{:S(2)}) copy-start(f32[1,64,8]{1,2,0:T(8,128)} %param.10) | copy-start | bytes 6148
  272.0 11.8 %copy-start.2 = (bf16[1,64,3584]{2,1,0:T(8,128)(2,1)S(1)}, bf16[1,64,3584]{2,1,0:T(8,128)(2,1)}, u32[]{:S(2)}) copy-start(bf16[1,64,3584]{2,1,0:T(8,128)(2,1)} %param.8) | copy-start | bytes 1376260
  272.0 126.9 %all-to-all-start.1 = ((bf16[128,5,2,3584]{3,2,1,0:T(2,128)(2,1)}), bf16[128,5,2,3584]{3,2,1,0:T(2,128)(2,1)}, u32[]{:S(2)}, u32[]{:S(2)}) async-start(bf16[128,5,2,3584]{3,2,1,0:T(2,128)(2,1)} %copy.33), calls=%async_computation.1 | async-start | bytes 18350080 | tf_op jit(solution)/shard_map/all_to_all | solution.py:80
  398.8 52.1 %slice-start = ((s8[7340032]{0:T(1024)(128)(4,1)}), s8[3145728]{0:T(1024)(128)(4,1)S(1)}, s32[]{:S(2)}) async-start(s8[7340032]{0:T(1024)(128)(4,1)} %bitcast.74), calls=%async_computation.2 | async-start | bytes 6291456
  428.2 22.6 %slice-start.1 = ((s8[7340032]{0:T(1024)(128)(4,1)}), s8[4194304]{0:T(1024)(128)(4,1)S(1)}, s32[]{:S(2)}) async-start(s8[7340032]{0:T(1024)(128)(4,1)} %bitcast.74), calls=%async_computation.3 | async-start | bytes 8388608
  443.5 7.4 %copy-start = (bf16[512,2,3584]{2,1,0:T(2,128)(2,1)S(1)}, bf16[512,2,3584]{2,1,0:T(2,128)(2,1)}, u32[]{:S(2)}) copy-start(bf16[512,2,3584]{2,1,0:T(2,128)(2,1)} %gather_fusion.1) | copy-start | bytes 22020100
where the time goes:
time: 491 us; the launch traced here: 482 us
  local copies, waits for them, and re-layouts  142 us (29%)
  blocking collectives  115 us (23%)
  waiting for transfers between devices  99.4 us (20%)
  matrix products  73.7 us (15%)
  other arithmetic  39.6 us (8%)
  starting transfers between devices  11.7 us (2%)
    all_to_all x1, blocking collectives, exchange_in_groups(): lax.all_to_all(group, axis, split_axis=split_dim, concat_axis=concat_dim,...  115 us
    all_to_all x1, waiting for transfers between devices, serve_rows(): lax.all_to_all(outcome.reshape(received.shape), ('cp', 'ep'), split_axis=...  99.4 us
    gather x1, local copies, waits for them, and re-layouts, per_device(): send_rows = stacked[slot_token]  31.5 us
    gather x1, local copies, waits for them, and re-layouts, per_device(): fetched = returned.reshape(owners * capacity, 2, features)[dest_slot]  29.4 us
    reduce_sum x1, other arithmetic, per_device(): jnp.sum(cotangent[0].astype(jnp.float32)[:, None, :] * expert_out, axis=-1)  27.7 us
    another operation x3, local copies, waits for them, and re-layouts, expert_rows(): return jnp.stack([expert_out, expert_grad], 1)  25.5 us
    dot_general x1, matrix products, expert_rows(): jnp.dot(grad_gate, gate_matrix.T, preferred_element_type=jnp.float32)  15.8 us
    mul x2, local copies, waits for them, and re-layouts, per_device(): cotangent[0].astype(jnp.float32)[:, None, :] * expert_out  15.6 us
  transfers between devices with their start and end apart: 1, of which 1 were waited for; matrix products, arithmetic and copies ran while one was open for 3% of the time, Pallas kernels for 0%

commit v1 on v0

v1 whole, which is shorter than its diff:
```python
import functools

import jax
import jax.numpy as jnp
from jax import lax
from jax.experimental import pallas as pl
from jax.experimental.pallas import tpu as pltpu
from jax.sharding import PartitionSpec as P

LANES = 128
GROUPS = ((0, 3), (3, 5))
AXES = ("cp", "ep")
F32 = jnp.float32
BF16 = jnp.bfloat16
ANY = pl.BlockSpec(memory_space=pl.ANY)
VMEM = pl.BlockSpec(memory_space=pltpu.VMEM)
SMEM = pl.BlockSpec(memory_space=pltpu.SMEM)


def pack_kernel(top_k, slots, tokens, cotangent, out, flat, records, sem):
    positions, features = tokens.shape
    cols = features // LANES
    height = 2 * cols
    for j in range(cols):
        lanes = slice(j * LANES, (j + 1) * LANES)
        flat[pl.ds(j, positions, stride=height), :] = tokens[:, lanes].astype(F32)
        flat[pl.ds(cols + j, positions, stride=height), :] = cotangent[:, lanes].astype(F32)
    records[0:positions] = flat[...].reshape(positions, height, LANES).astype(BF16)
    records[positions] = jnp.zeros((height, LANES), BF16)

    @pl.loop(0, out.shape[0], unroll=8)
    def _(r):
        pltpu.make_async_copy(records.at[slots[r] // top_k], out.at[r], sem).start()

    pltpu.make_async_copy(out, out, sem).wait()


def pack(slots, tokens, cotangent, top_k):
    positions, features = tokens.shape
    height = 2 * features // LANES
    rows = slots.shape[0]
    return pl.pallas_call(
        functools.partial(pack_kernel, top_k),
        out_shape=jax.ShapeDtypeStruct((rows, height, LANES), BF16),
        in_specs=[SMEM, VMEM, VMEM],
        out_specs=ANY,
        scratch_shapes=[
            pltpu.VMEM((positions * height, LANES), F32),
            pltpu.VMEM((positions + 1, height, LANES), BF16),
            pltpu.SemaphoreType.DMA,
        ],
        cost_estimate=pl.CostEstimate(
            flops=0, transcendentals=0, bytes_accessed=rows * height * LANES * 4
        ),
        name="pack",
    )(slots, tokens, cotangent)


NT = (((1,), (1,)), ((), ()))


def expert_kernel(
    rec_in, w_gate, w_up, w_down, rec_out,
    rec, wg, wu, wd, inputs, grads, hidden, grad_gate, grad_up, flat, sems,
):
    rows, height, _ = rec.shape
    features, width = wg.shape
    cols = height // 2
    copies = [
        pltpu.make_async_copy(src, dst, sems.at[i])
        for i, (src, dst) in enumerate(
            ((rec_in, rec), (w_gate, wg), (w_up, wu), (w_down, wd))
        )
    ]
    for c in copies:
        c.start()
    copies[0].wait()
    step = 64

    @pl.loop(0, rows // step)
    def _(c):
        first = pl.multiple_of(c * step, step)
        part = flat.at[pl.ds(0, step * height)]
        part[...] = rec[pl.ds(first, step)].astype(F32).reshape(step * height, LANES)
        for j in range(cols):
            lanes = slice(j * LANES, (j + 1) * LANES)
            inputs[pl.ds(first, step), lanes] = part[pl.ds(j, step, stride=height), :].astype(BF16)
            grads[pl.ds(first, step), lanes] = part[
                pl.ds(cols + j, step, stride=height), :
            ].astype(BF16)

    for c in copies[1:]:
        c.wait()
    block = 256
    for h in range(width // block):
        part = slice(h * block, (h + 1) * block)
        gate_pre = jnp.dot(inputs[...], wg[:, part], preferred_element_type=F32)
        up_pre = jnp.dot(inputs[...], wu[:, part], preferred_element_type=F32)
        grad_hidden = lax.dot_general(grads[...], wd[part, :], NT, preferred_element_type=F32)
        sig = jax.nn.sigmoid(gate_pre)
        silu = gate_pre * sig
        hidden[:, part] = (silu * up_pre).astype(BF16)
        grad_gate[:, part] = (grad_hidden * up_pre * sig * (1.0 + gate_pre * (1.0 - sig))).astype(BF16)
        grad_up[:, part] = (grad_hidden * silu).astype(BF16)
    for h in range(features // block):
        part = slice(h * block, (h + 1) * block)
        expert_out = jnp.dot(hidden[...], wd[:, part], preferred_element_type=F32)
        expert_grad = lax.dot_general(
            grad_gate[...], wg[part, :], NT, preferred_element_type=F32
        ) + lax.dot_general(grad_up[...], wu[part, :], NT, preferred_element_type=F32)
        for j in range(block // LANES):
            at = h * (block // LANES) + j
            lanes = slice(j * LANES, (j + 1) * LANES)
            flat[pl.ds(at, rows, stride=height), :] = expert_out[:, lanes]
            flat[pl.ds(cols + at, rows, stride=height), :] = expert_grad[:, lanes]

    @pl.loop(0, rows // step)
    def _(c):
        first = pl.multiple_of(c * step, step)
        source = flat[pl.ds(pl.multiple_of(first * height, step * height), step * height), :]
        rec[pl.ds(first, step)] = source.reshape(step, height, LANES).astype(BF16)
        pltpu.make_async_copy(
            rec.at[pl.ds(first, step)], rec_out.at[pl.ds(first, step)], sems.at[0]
        ).start()

    pltpu.make_async_copy(rec, rec_out, sems.at[0]).wait()


def expert(records, w_gate, w_up, w_down):
    rows, height, _ = records.shape
    features, width = w_gate.shape
    return pl.pallas_call(
        expert_kernel,
        out_shape=jax.ShapeDtypeStruct(records.shape, BF16),
        in_specs=[ANY] * 4,
        out_specs=ANY,
        scratch_shapes=[
            pltpu.VMEM((rows, height, LANES), BF16),
            pltpu.VMEM((features, width), BF16),
            pltpu.VMEM((features, width), BF16),
            pltpu.VMEM((width, features), BF16),
            pltpu.VMEM((rows, features), BF16),
            pltpu.VMEM((rows, features), BF16),
            pltpu.VMEM((rows, width), BF16),
            pltpu.VMEM((rows, width), BF16),
            pltpu.VMEM((rows, width), BF16),
            pltpu.VMEM((rows * height, LANES), F32),
            pltpu.SemaphoreType.DMA((4,)),
        ],
        cost_estimate=pl.CostEstimate(
            flops=12 * rows * features * width,
            transcendentals=rows * width,
            bytes_accessed=6 * features * width + 4 * rows * height * LANES,
        ),
        compiler_params=pltpu.CompilerParams(vmem_limit_bytes=60 * 1024 * 1024),
        name="expert",
    )(records, w_gate, w_up, w_down)


def unpack_kernel(
    first, last, top_k, slots, weights, rec_in, cotangent, acc_in, dots_in, *rest
):
    if last:
        layer_out, token_grad, gate_grad, rec, acc, dots, cot, sems = rest
    else:
        acc, dots, rec, cot, sems = rest
    positions, features = cotangent.shape
    rows, height, _ = rec.shape
    cols = features // LANES
    load = pltpu.make_async_copy(rec_in, rec, sems.at[0])
    load.start()
    for j in range(cols):
        cot[pl.ds(j, positions, stride=cols), :] = cotangent[:, j * LANES : (j + 1) * LANES].astype(F32)
    if first:
        acc[...] = jnp.zeros_like(acc)
        dots[...] = jnp.zeros_like(dots)
    else:
        acc[...] = acc_in[...]
        dots[...] = dots_in[...]
    load.wait()

    @pl.loop(0, rows)
    def _(r):
        slot = slots[r]

        @pl.when(slot < positions * top_k)
        def _():
            token = slot // top_k
            value = rec[r].astype(F32)
            acc[token] += weights[slot] * value
            at = pl.multiple_of(token * cols, 4)
            product = cot[pl.ds(at, cols), :] * value[:cols]
            dots[pl.ds(slot, 1), :] = jnp.sum(product, axis=0, keepdims=True)

    if last:
        lane = lax.broadcasted_iota(jnp.int32, (positions, top_k), 1)
        grads = jnp.zeros((positions, top_k), F32)
        for k in range(top_k):
            column = jnp.sum(dots[pl.ds(k, positions, stride=top_k), :], axis=1, keepdims=True)
            grads = jnp.where(lane == k, column, grads)
        gate_grad[...] = grads
        flat = acc.reshape((positions + 1) * height, LANES)
        for j in range(cols):
            lanes = slice(j * LANES, (j + 1) * LANES)
            layer_out[:, lanes] = flat[pl.ds(j, positions, stride=height), :].astype(BF16)
            token_grad[:, lanes] = flat[pl.ds(cols + j, positions, stride=height), :].astype(BF16)


def unpack(slots, weights, records, cotangent, carry, last, top_k):
    positions, features = cotangent.shape
    rows, height, _ = records.shape
    acc_shape = (positions + 1, height, LANES)
    dots_shape = (positions * top_k, LANES)
    first = carry is None
    if first:
        carry = (jnp.zeros((8, LANES), F32), jnp.zeros((8, LANES), F32))
    scratch = [
        pltpu.VMEM((rows, height, LANES), BF16),
        pltpu.VMEM((positions * features // LANES, LANES), F32),
        pltpu.SemaphoreType.DMA((1,)),
    ]
    if last:
        out_shape = (
            jax.ShapeDtypeStruct((positions, features), BF16),
            jax.ShapeDtypeStruct((positions, features), BF16),
            jax.ShapeDtypeStruct((positions, top_k), F32),
        )
        scratch[1:1] = [pltpu.VMEM(acc_shape, F32), pltpu.VMEM(dots_shape, F32)]
    else:
        out_shape = (
            jax.ShapeDtypeStruct(acc_shape, F32),
            jax.ShapeDtypeStruct(dots_shape, F32),
        )
    return pl.pallas_call(
        functools.partial(unpack_kernel, first, last, top_k),
        out_shape=out_shape,
        in_specs=[SMEM, SMEM, ANY, VMEM, VMEM, VMEM],
        out_specs=tuple(VMEM for _ in out_shape),
        scratch_shapes=scratch,
        cost_estimate=pl.CostEstimate(
            flops=8 * rows * height * LANES,
            transcendentals=0,
            bytes_accessed=rows * height * LANES * 4,
        ),
        name="unpack",
    )(slots, weights, records, cotangent, *carry)


def exchange(value):
    return lax.all_to_all(value, AXES, split_axis=0, concat_axis=0, tiled=True)


def per_device(tokens, cotangent, routes, router_weights, w_gate, w_up, w_down):
    owners = lax.axis_size("cp") * lax.axis_size("ep")
    positions = tokens.shape[1]
    top_k = routes.shape[2]
    count = positions * top_k
    capacity = count // owners * 5 // 4
    flat_routes = routes[0].reshape(count)
    index = jnp.arange(count, dtype=jnp.int32)
    earlier = (flat_routes[None, :] == flat_routes[:, None]) & (index[None, :] < index[:, None])
    rank = jnp.sum(earlier.astype(jnp.int32), axis=1)
    place = flat_routes * capacity + rank
    holds = place[None, :] == jnp.arange(owners * capacity, dtype=jnp.int32)[:, None]
    slot_of = count + jnp.sum(jnp.where(holds, index[None, :] - count, 0), axis=1)
    slot_of = slot_of.reshape(owners, capacity)
    weights = router_weights[0].reshape(count)

    slots = [slot_of[:, a:b].reshape(owners * (b - a)) for a, b in GROUPS]
    sent = [pack(s, tokens[0], cotangent[0], top_k) for s in slots]
    arrived = [exchange(s) for s in sent]
    done = [expert(a, w_gate[0], w_up[0], w_down[0]) for a in arrived]
    returned = [exchange(d) for d in done]
    carry = None
    for i, (s, r) in enumerate(zip(slots, returned)):
        carry = unpack(s, weights, r, cotangent[0], carry, i == len(GROUPS) - 1, top_k)
    layer_out, token_grad, gate_grad = carry
    return layer_out[None], token_grad[None], gate_grad[None]


def solution(mesh):
    in_specs = (
        P("ep", "cp", None),
        P("ep", "cp", None),
        P("ep", "cp", None),
        P("ep", "cp", None),
        P(("cp", "ep"), None, None),
        P(("cp", "ep"), None, None),
        P(("cp", "ep"), None, None),
    )
    out_specs = (P("ep", "cp", None), P("ep", "cp", None), P("ep", "cp", None))
    return jax.shard_map(
        per_device, mesh=mesh, in_specs=in_specs, out_specs=out_specs, check_vma=False
    )
```

time: 491 us -> 282 us (0.57); the launches traced: 482 us -> 278 us
  local copies, waits for them, and re-layouts: 142 us -> 5.44 us
  blocking collectives: 115 us -> 0 us
  Pallas kernels: 0 us -> 85.8 us
  matrix products: 73.7 us -> 0 us
  waiting for transfers between devices: 99.4 us -> 150 us
  other arithmetic: 39.6 us -> 0.48 us
  starting transfers between devices: 11.7 us -> 35.1 us
    all_to_all x1 -> x0, blocking collectives: 115 us -> none  [exchange_in_groups(): lax.all_to_all(group, axis, split_axis=split_dim, concat_axis=concat_dim,...]
    pallas_call x0 -> x6, Pallas kernels: none -> 85.8 us  [the longest x2 51.8 us: expert(): pl.pallas_call(expert_kernel, out_shape=jax.ShapeDtypeStruct(records.shap...]
    dot_general x8 -> x0, matrix products: 73.7 us -> none  [the longest x1 15.8 us: expert_rows(): jnp.dot(grad_gate, gate_matrix.T, preferred_element_type=jnp.float32)]
    gather x2 -> x0, local copies, waits for them, and re-layouts: 60.9 us -> none  [the longest x1 31.5 us: per_device(): send_rows = stacked[slot_token]]
    all_to_all x1 -> x4, waiting for transfers between devices: 99.4 us -> 150 us  [exchange(): return lax.all_to_all(value, AXES, split_axis=0, concat_axis=0, tiled=True)]
    slice x2 -> x1, local copies, waits for them, and re-layouts: 29 us -> 0.08 us  [per_device(): slots = [slot_of[:, a:b].reshape(owners * (b - a)) for a, b in GROUPS]]
    another operation x8 -> x3, local copies, waits for them, and re-layouts: 29 us -> 1.37 us  [the longest x1 0.69 us: per_device(): weights = router_weights[0].reshape(count)]
    reduce_sum x2, other arithmetic: 27.9 us -> 0.47 us  [the longest x1 0.25 us: per_device(): rank = jnp.sum(earlier.astype(jnp.int32), axis=1)]
  transfers between devices with their start and end apart: 1 -> 4, of which waited for: 1 -> 4; matrix products, arithmetic and copies ran while one was open for 3% -> 1% of each run, Pallas kernels for 0% -> 25%
where the time goes in v1:
time: 282 us; the launch traced here: 278 us
  waiting for transfers between devices  150 us (53%)
  Pallas kernels  85.8 us (30%)
  starting transfers between devices  35.1 us (12%)
  local copies, waits for them, and re-layouts  5.44 us (2%)
    all_to_all x4, waiting for transfers between devices, exchange(): return lax.all_to_all(value, AXES, split_axis=0, concat_axis=0, tiled=True)  150 us
    pallas_call x2, Pallas kernels, expert(): pl.pallas_call(expert_kernel, out_shape=jax.ShapeDtypeStruct(records.shap...  51.8 us
    all_to_all x4, starting transfers between devices, exchange(): return lax.all_to_all(value, AXES, split_axis=0, concat_axis=0, tiled=True)  35.1 us
    pallas_call x2, Pallas kernels, unpack(): pl.pallas_call(functools.partial(unpack_kernel, first, last, top_k), out_...  25.1 us
    pallas_call x2, Pallas kernels, pack(): pl.pallas_call(functools.partial(pack_kernel, top_k), out_shape=jax.Shape...  8.87 us
  transfers between devices with their start and end apart: 4, of which 4 were waited for; matrix products, arithmetic and copies ran while one was open for 1% of the time, Pallas kernels for 25%

profile of v1, /device:TPU:34, one launch (start us, length us, event | category | flops | bytes accessed | tf_op | source)
XLA Modules:
  0.0 278.0 jit_solution(10645456590468774557)
XLA Ops:
  0.6 0.8 copy.14
  1.4 0.1 reshape_squeeze.6
  1.5 0.3 convert_reduce_fusion
  1.8 0.2 select_reduce_fusion
  2.0 0.2 add.26
  2.2 0.8 reshape.32.slots
  3.0 4.9 %pack.3 = bf16[384,56,128]{2,1,0:T(8,128)(2,1)} custom-call(s32[384]{0:T(512)} %reshape.32.slots, bf16[64,3584]{1,0:T(8,128)(2,1)} %bitcast.13, bf16[64,3584]{1,0:T(8,128)(2,1)} %bitcast.9), custom_call_target="tpu_custom_call" | custom-call | bytes 11010048 | tf_op jit(solution)/shard_map/pack/pallas_call | solution.py:42
  7.9 10.6 %all-to-all-start.2 = ((bf16[384,56,128]{2,1,0:T(8,128)(2,1)}), bf16[384,56,128]{2,1,0:T(8,128)(2,1)}, u32[]{:S(2)}, u32[]{:S(2)}) async-start(bf16[384,56,128]{2,1,0:T(8,128)(2,1)} %pack.3), calls=%async_computation.2 | async-start | bytes 11010048 | tf_op jit(solution)/shard_map/all_to_all | solution.py:250
  18.5 0.1 slice.8
  18.6 0.7 reshape.31.slots
  19.3 4.0 %pack.2 = bf16[256,56,128]{2,1,0:T(8,128)(2,1)} custom-call(s32[256]{0:T(256)} %reshape.31.slots, bf16[64,3584]{1,0:T(8,128)(2,1)} %bitcast.14, bf16[64,3584]{1,0:T(8,128)(2,1)} %bitcast.10), custom_call_target="tpu_custom_call" | custom-call | bytes 7340032 | tf_op jit(solution)/shard_map/pack/pallas_call | solution.py:42
  23.3 61.9 %all-to-all-done.2.rec_in = bf16[384,56,128]{2,1,0:T(8,128)(2,1)} async-done(((bf16[384,56,128]{2,1,0:T(8,128)(2,1)}), bf16[384,56,128]{2,1,0:T(8,128)(2,1)}, u32[]{:S(2)}, u32[]{:S(2)}) %all-to-all-start.2) | async-done | bytes 5505056 | tf_op jit(solution)/shard_map/all_to_all | solution.py:250
  85.2 8.4 %all-to-all-start = ((bf16[256,56,128]{2,1,0:T(8,128)(2,1)}), bf16[256,56,128]{2,1,0:T(8,128)(2,1)}, u32[]{:S(2)}, u32[]{:S(2)}) async-start(bf16[256,56,128]{2,1,0:T(8,128)(2,1)} %pack.2), calls=%async_computation | async-start | bytes 7340032 | tf_op jit(solution)/shard_map/all_to_all | solution.py:250
  93.6 29.4 %expert.3 = bf16[384,56,128]{2,1,0:T(8,128)(2,1)} custom-call(bf16[384,56,128]{2,1,0:T(8,128)(2,1)} %all-to-all-done.2.rec_in, bf16[3584,1024]{1,0:T(8,128)(2,1)} %bitcast.17, bf16[3584,1024]{1,0:T(8,128)(2,1)} %bitcast.19, bf16[1024,3584]{1,0:T(8,128)(2,1)} %bitcast.21), custom_call_target="tpu_custom_call" | custom-call | flops 16911433728 | bytes 33030144 | tf_op jit(solution)/shard_map/expert/pallas_call | solution.py:132
  123.0 15.6 %all-to-all-done.rec_in = bf16[256,56,128]{2,1,0:T(8,128)(2,1)} async-done(((bf16[256,56,128]{2,1,0:T(8,128)(2,1)}), bf16[256,56,128]{2,1,0:T(8,128)(2,1)}, u32[]{:S(2)}, u32[]{:S(2)}) %all-to-all-start) | async-done | bytes 3670048 | tf_op jit(solution)/shard_map/all_to_all | solution.py:250
  138.6 7.8 %all-to-all-start.3 = ((bf16[384,56,128]{2,1,0:T(8,128)(2,1)}), bf16[384,56,128]{2,1,0:T(8,128)(2,1)}, u32[]{:S(2)}, u32[]{:S(2)}) async-start(bf16[384,56,128]{2,1,0:T(8,128)(2,1)} %expert.3), calls=%async_computation.3 | async-start | bytes 11010048 | tf_op jit(solution)/shard_map/all_to_all | solution.py:250
  146.4 22.4 %expert.2 = bf16[256,56,128]{2,1,0:T(8,128)(2,1)} custom-call(bf16[256,56,128]{2,1,0:T(8,128)(2,1)} %all-to-all-done.rec_in, bf16[3584,1024]{1,0:T(8,128)(2,1)} %bitcast.18, bf16[3584,1024]{1,0:T(8,128)(2,1)} %bitcast.20, bf16[1024,3584]{1,0:T(8,128)(2,1)} %bitcast.22), custom_call_target="tpu_custom_call" | custom-call | flops 11274289152 | bytes 29360128 | tf_op jit(solution)/shard_map/expert/pallas_call | solution.py:132
  168.8 0.0 copy-start
  168.8 44.3 %all-to-all-done.3.rec_in = bf16[384,56,128]{2,1,0:T(8,128)(2,1)} async-done(((bf16[384,56,128]{2,1,0:T(8,128)(2,1)}), bf16[384,56,128]{2,1,0:T(8,128)(2,1)}, u32[]{:S(2)}, u32[]{:S(2)}) %all-to-all-start.3) | async-done | bytes 5505056 | tf_op jit(solution)/shard_map/all_to_all | solution.py:250
  213.1 8.4 %all-to-all-start.1 = ((bf16[256,56,128]{2,1,0:T(8,128)(2,1)}), bf16[256,56,128]{2,1,0:T(8,128)(2,1)}, u32[]{:S(2)}, u32[]{:S(2)}) async-start(bf16[256,56,128]{2,1,0:T(8,128)(2,1)} %expert.2), calls=%async_computation.1 | async-start | bytes 7340032 | tf_op jit(solution)/shard_map/all_to_all | solution.py:250
  221.5 0.0 copy-done
  221.5 0.1 copy.15
  221.6 0.7 reshape_squeeze.7.weights
  222.2 0.6 broadcast_1_acc_in_dots_in.2.acc_in.dots_in
  222.8 15.0 %unpack.2 = (f32[65,56,128]{2,1,0:T(8,128)}, f32[512,128]{1,0:T(8,128)}) custom-call(s32[384]{0:T(512)} %reshape.32.slots, f32[512]{0:T(512)} %reshape_squeeze.7.weights, bf16[384,56,128]{2,1,0:T(8,128)(2,1)} %all-to-all-done.3.rec_in, bf16[64,3584]{1,0:T(8,128)(2,1)} %bitcast.11, f32[8,128]{1,0:T(8,128)} %broadcast_1_acc_in_dots_in.2.acc_in.dots_in, ...), custom_call_target="tpu_custom_call" | custom-call | flops 22020096 | bytes 11010048 | tf_op jit(solution)/shard_map/unpack/pallas_call | solution.py:234
  237.8 28.6 %all-to-all-done.1.rec_in = bf16[256,56,128]{2,1,0:T(8,128)(2,1)} async-done(((bf16[256,56,128]{2,1,0:T(8,128)(2,1)}), bf16[256,56,128]{2,1,0:T(8,128)(2,1)}, u32[]{:S(2)}, u32[]{:S(2)}) %all-to-all-start.1) | async-done | bytes 3670048 | tf_op jit(solution)/shard_map/all_to_all | solution.py:250
  266.4 10.1 %unpack.3 = (bf16[64,3584]{1,0:T(8,128)(2,1)}, bf16[64,3584]{1,0:T(8,128)(2,1)}, f32[64,8]{1,0:T(8,128)}) custom-call(s32[256]{0:T(256)} %reshape.31.slots, f32[512]{0:T(512)} %reshape_squeeze.7.weights, bf16[256,56,128]{2,1,0:T(8,128)(2,1)} %all-to-all-done.1.rec_in, bf16[64,3584]{1,0:T(8,128)(2,1)} %bitcast.12, f32[65,56,128]{2,1,0:T(8,128)} %get-tuple-element.8.acc_in, ...), custom_call_target="tpu_custom_call" | custom-call | flops 14680064 | bytes 7340032 | tf_op jit(solution)/shard_map/unpack/pallas_call | solution.py:234
  276.6 1.4 copy.16
  (2 shorter events, 0.0 us)
Async XLA Ops:
  7.9 77.4 %all-to-all-start.2 = ((bf16[384,56,128]{2,1,0:T(8,128)(2,1)}), bf16[384,56,128]{2,1,0:T(8,128)(2,1)}, u32[]{:S(2)}, u32[]{:S(2)}) async-start(bf16[384,56,128]{2,1,0:T(8,128)(2,1)} %pack.3), calls=%async_computation.2 | async-start | bytes 11010048 | tf_op jit(solution)/shard_map/all_to_all | solution.py:250
  85.2 53.4 %all-to-all-start = ((bf16[256,56,128]{2,1,0:T(8,128)(2,1)}), bf16[256,56,128]{2,1,0:T(8,128)(2,1)}, u32[]{:S(2)}, u32[]{:S(2)}) async-start(bf16[256,56,128]{2,1,0:T(8,128)(2,1)} %pack.2), calls=%async_computation | async-start | bytes 7340032 | tf_op jit(solution)/shard_map/all_to_all | solution.py:250
  138.6 74.5 %all-to-all-start.3 = ((bf16[384,56,128]{2,1,0:T(8,128)(2,1)}), bf16[384,56,128]{2,1,0:T(8,128)(2,1)}, u32[]{:S(2)}, u32[]{:S(2)}) async-start(bf16[384,56,128]{2,1,0:T(8,128)(2,1)} %expert.3), calls=%async_computation.3 | async-start | bytes 11010048 | tf_op jit(solution)/shard_map/all_to_all | solution.py:250
  168.8 52.7 %copy-start = (f32[1,64,8]{1,2,0:T(8,128)S(1)}, f32[1,64,8]{1,2,0:T(8,128)}, u32[]{:S(2)}) copy-start(f32[1,64,8]{1,2,0:T(8,128)} %param.10) | copy-start | bytes 6148
  213.1 53.3 %all-to-all-start.1 = ((bf16[256,56,128]{2,1,0:T(8,128)(2,1)}), bf16[256,56,128]{2,1,0:T(8,128)(2,1)}, u32[]{:S(2)}, u32[]{:S(2)}) async-start(bf16[256,56,128]{2,1,0:T(8,128)(2,1)} %expert.2), calls=%async_computation.1 | async-start | bytes 7340032 | tf_op jit(solution)/shard_map/all_to_all | solution.py:250

commit v2 on v1

--- a/solution.py
+++ b/solution.py
@@ -10,6 +10,8 @@
 LANES = 128
 GROUPS = ((0, 3), (3, 5))
 AXES = ("cp", "ep")
+SPAN = 128
+EMPTY = 8 * SPAN + 64
 F32 = jnp.float32
 BF16 = jnp.bfloat16
 ANY = pl.BlockSpec(memory_space=pl.ANY)
@@ -17,7 +19,30 @@
 SMEM = pl.BlockSpec(memory_space=pltpu.SMEM)
 
 
-def pack_kernel(top_k, slots, tokens, cotangent, out, flat, records, sem):
+def route(routes, positions, owners):
+    top_k = routes.shape[0]
+    by_token = routes[...].astype(F32).T
+    lane = lax.broadcasted_iota(jnp.int32, (positions, owners), 1).astype(F32)
+    token = lax.broadcasted_iota(jnp.int32, (positions, owners), 0).astype(F32)
+    named = jnp.zeros((positions, owners), F32)
+    slot = token - EMPTY
+    for k in range(top_k):
+        match = by_token[:, k : k + 1] == lane
+        named = jnp.where(match, 1.0, named)
+        slot = jnp.where(match, slot + k * SPAN, slot)
+    row = lax.broadcasted_iota(jnp.int32, (positions, positions), 0)
+    col = lax.broadcasted_iota(jnp.int32, (positions, positions), 1)
+    before = jnp.where(col < row, 1.0, 0.0).astype(BF16)
+    rank = jnp.dot(before, named.astype(BF16), preferred_element_type=F32)
+    rank = jnp.where(named > 0.0, rank, -1.0)
+    rows = [
+        jnp.sum(jnp.where(rank == float(i), slot, 0.0), axis=0, keepdims=True) + EMPTY
+        for i in range(8)
+    ]
+    return jnp.concatenate(rows, axis=0).astype(jnp.int32)
+
+
+def build_records(tokens, cotangent, flat, records):
     positions, features = tokens.shape
     cols = features // LANES
     height = 2 * cols
@@ -28,19 +53,90 @@
     records[0:positions] = flat[...].reshape(positions, height, LANES).astype(BF16)
     records[positions] = jnp.zeros((height, LANES), BF16)
 
-    @pl.loop(0, out.shape[0], unroll=8)
-    def _(r):
-        pltpu.make_async_copy(records.at[slots[r] // top_k], out.at[r], sem).start()
+
+def send_records(group, table, records, out, sem):
+    first, last = group
+    span = last - first
+
+    @pl.loop(0, out.shape[0] // span, unroll=4)
+    def _(e):
+        for i in range(span):
+            token = table[first + i, e] & (SPAN - 1)
+            pltpu.make_async_copy(records.at[token], out.at[e * span + i], sem).start()
 
     pltpu.make_async_copy(out, out, sem).wait()
 
 
-def pack(slots, tokens, cotangent, top_k):
+def first_pack_kernel(
+    group, routes, tokens_in, cotangent_in, out, table_out,
+    tokens, cotangent, table, table_smem, flat, records, sem, sems,
+):
+    positions = tokens.shape[0]
+    load = [
+        pltpu.make_async_copy(tokens_in, tokens, sems.at[0]),
+        pltpu.make_async_copy(cotangent_in, cotangent, sems.at[1]),
+    ]
+    for c in load:
+        c.start()
+    table[...] = route(routes, positions, table.shape[1])
+    keep = [
+        pltpu.make_async_copy(table, table_smem, sems.at[2]),
+        pltpu.make_async_copy(table, table_out, sems.at[3]),
+    ]
+    for c in keep:
+        c.start()
+    for c in load:
+        c.wait()
+    build_records(tokens, cotangent, flat, records)
+    for c in keep:
+        c.wait()
+    send_records(group, table_smem, records, out, sem)
+
+
+def next_pack_kernel(group, table, tokens, cotangent, out, flat, records, sem):
+    build_records(tokens, cotangent, flat, records)
+    send_records(group, table, records, out, sem)
+
+
+def pack_cost(rows, height):
+    return pl.CostEstimate(
+        flops=0, transcendentals=0, bytes_accessed=rows * height * LANES * 4
+    )
+
+
+def first_pack(group, routes, tokens, cotangent, owners):
     positions, features = tokens.shape
     height = 2 * features // LANES
-    rows = slots.shape[0]
+    rows = owners * (group[1] - group[0])
     return pl.pallas_call(
-        functools.partial(pack_kernel, top_k),
+        functools.partial(first_pack_kernel, group),
+        out_shape=(
+            jax.ShapeDtypeStruct((rows, height, LANES), BF16),
+            jax.ShapeDtypeStruct((8, owners), jnp.int32),
+        ),
+        in_specs=[VMEM, ANY, ANY],
+        out_specs=(ANY, ANY),
+        scratch_shapes=[
+            pltpu.VMEM((positions, features), BF16),
+            pltpu.VMEM((positions, features), BF16),
+            pltpu.VMEM((8, owners), jnp.int32),
+            pltpu.SMEM((8, owners), jnp.int32),
+            pltpu.VMEM((positions * height, LANES), F32),
+            pltpu.VMEM((positions + 1, height, LANES), BF16),
+            pltpu.SemaphoreType.DMA,
+            pltpu.SemaphoreType.DMA((4,)),
+        ],
+        cost_estimate=pack_cost(rows, height),
+        name="first_pack",
+    )(routes, tokens, cotangent)
+
+
+def next_pack(group, table, tokens, cotangent):
+    positions, features = tokens.shape
+    height = 2 * features // LANES
+    rows = table.shape[1] * (group[1] - group[0])
+    return pl.pallas_call(
+        functools.partial(next_pack_kernel, group),
         out_shape=jax.ShapeDtypeStruct((rows, height, LANES), BF16),
         in_specs=[SMEM, VMEM, VMEM],
         out_specs=ANY,
@@ -49,11 +145,9 @@
             pltpu.VMEM((positions + 1, height, LANES), BF16),
             pltpu.SemaphoreType.DMA,
         ],
-        cost_estimate=pl.CostEstimate(
-            flops=0, transcendentals=0, bytes_accessed=rows * height * LANES * 4
-        ),
-        name="pack",
-    )(slots, tokens, cotangent)
+        cost_estimate=pack_cost(rows, height),
+        name="next_pack",
+    )(table, tokens, cotangent)
 
 
 NT = (((1,), (1,)), ((), ()))
@@ -157,93 +251,126 @@
     )(records, w_gate, w_up, w_down)
 
 
-def unpack_kernel(
-    first, last, top_k, slots, weights, rec_in, cotangent, acc_in, dots_in, *rest
-):
+def unpack_kernel(group, first, last, table, weights, rec_in, cotangent_in, *rest):
+    if not first:
+        acc_in, dots_in, *rest = rest
     if last:
-        layer_out, token_grad, gate_grad, rec, acc, dots, cot, sems = rest
+        layer_out, token_grad, gate_grad, *rest = rest
     else:
-        acc, dots, rec, cot, sems = rest
+        acc_out, dots_out, *rest = rest
+    rec, cotangent, cot, acc, dots, sems = rest
     positions, features = cotangent.shape
     rows, height, _ = rec.shape
+    top_k = weights.shape[0]
     cols = features // LANES
-    load = pltpu.make_async_copy(rec_in, rec, sems.at[0])
-    load.start()
-    for j in range(cols):
-        cot[pl.ds(j, positions, stride=cols), :] = cotangent[:, j * LANES : (j + 1) * LANES].astype(F32)
+    chunks = sems.shape[0] - 3
+    part = rows // chunks
+    loads = [
+        pltpu.make_async_copy(
+            rec_in.at[pl.ds(c * part, part)], rec.at[pl.ds(c * part, part)], sems.at[3 + c]
+        )
+        for c in range(chunks)
+    ]
+    others = [pltpu.make_async_copy(cotangent_in, cotangent, sems.at[0])]
+    if not first:
+        others.append(pltpu.make_async_copy(acc_in, acc, sems.at[1]))
+        others.append(pltpu.make_async_copy(dots_in, dots, sems.at[2]))
+    for c in others[:1] + loads[:1] + others[1:] + loads[1:]:
+        c.start()
     if first:
         acc[...] = jnp.zeros_like(acc)
         dots[...] = jnp.zeros_like(dots)
-    else:
-        acc[...] = acc_in[...]
-        dots[...] = dots_in[...]
-    load.wait()
-
-    @pl.loop(0, rows)
-    def _(r):
-        slot = slots[r]
-
-        @pl.when(slot < positions * top_k)
-        def _():
-            token = slot // top_k
-            value = rec[r].astype(F32)
-            acc[token] += weights[slot] * value
-            at = pl.multiple_of(token * cols, 4)
-            product = cot[pl.ds(at, cols), :] * value[:cols]
-            dots[pl.ds(slot, 1), :] = jnp.sum(product, axis=0, keepdims=True)
+    cot[...] = jnp.zeros_like(cot)
+    tall = cot.shape[1]
+    flat_cot = cot.reshape(cot.shape[0] * tall, LANES)
+    others[0].wait()
+    for j in range(cols):
+        flat_cot[pl.ds(j, positions, stride=tall), :] = cotangent[
+            :, j * LANES : (j + 1) * LANES
+        ].astype(F32)
+    for c in others[1:]:
+        c.wait()
+    span = group[1] - group[0]
+    together = 2 * span
+
+    for c in range(chunks):
+        loads[c].wait()
+
+        @pl.loop(0, part // together)
+        def _(step):
+            todo = []
+            for u in range(together):
+                r = c * part + step * together + u
+                expert_at = c * (part // span) + step * 2 + u // span
+                slot = table[group[0] + u % span, expert_at]
+                token = slot & (SPAN - 1)
+                k = slot // SPAN
+                weight = weights[k & (top_k - 1), token & (positions - 1)]
+                value = rec[r].astype(F32)
+                dot = jnp.sum(cot[token] * value[:tall], axis=0, keepdims=True)
+                todo.append((token, k * positions + token, weight * value, dot))
+            for token, at, scaled, dot in todo:
+                acc[token] += scaled
+                dots[pl.ds(at, 1), :] = dot
 
     if last:
-        lane = lax.broadcasted_iota(jnp.int32, (positions, top_k), 1)
-        grads = jnp.zeros((positions, top_k), F32)
-        for k in range(top_k):
-            column = jnp.sum(dots[pl.ds(k, positions, stride=top_k), :], axis=1, keepdims=True)
-            grads = jnp.where(lane == k, column, grads)
-        gate_grad[...] = grads
+        gate_grad[...] = jnp.sum(
+            dots[0 : top_k * positions].reshape(top_k, positions, LANES), axis=2
+        )
         flat = acc.reshape((positions + 1) * height, LANES)
         for j in range(cols):
             lanes = slice(j * LANES, (j + 1) * LANES)
             layer_out[:, lanes] = flat[pl.ds(j, positions, stride=height), :].astype(BF16)
             token_grad[:, lanes] = flat[pl.ds(cols + j, positions, stride=height), :].astype(BF16)
-
-
-def unpack(slots, weights, records, cotangent, carry, last, top_k):
+    else:
+        stores = [
+            pltpu.make_async_copy(acc, acc_out, sems.at[1]),
+            pltpu.make_async_copy(dots, dots_out, sems.at[2]),
+        ]
+        for c in stores:
+            c.start()
+        for c in stores:
+            c.wait()
+
+
+def unpack(group, table, weights, records, cotangent, carry, last):
     positions, features = cotangent.shape
     rows, height, _ = records.shape
+    top_k = weights.shape[0]
+    cols = features // LANES
     acc_shape = (positions + 1, height, LANES)
-    dots_shape = (positions * top_k, LANES)
-    first = carry is None
-    if first:
-        carry = (jnp.zeros((8, LANES), F32), jnp.zeros((8, LANES), F32))
-    scratch = [
-        pltpu.VMEM((rows, height, LANES), BF16),
-        pltpu.VMEM((positions * features // LANES, LANES), F32),
-        pltpu.SemaphoreType.DMA((1,)),
-    ]
+    dots_shape = (top_k * positions + positions + 8, LANES)
     if last:
         out_shape = (
             jax.ShapeDtypeStruct((positions, features), BF16),
             jax.ShapeDtypeStruct((positions, features), BF16),
-            jax.ShapeDtypeStruct((positions, top_k), F32),
+            jax.ShapeDtypeStruct((top_k, positions), F32),
         )
-        scratch[1:1] = [pltpu.VMEM(acc_shape, F32), pltpu.VMEM(dots_shape, F32)]
     else:
         out_shape = (
             jax.ShapeDtypeStruct(acc_shape, F32),
             jax.ShapeDtypeStruct(dots_shape, F32),
         )
     return pl.pallas_call(
-        functools.partial(unpack_kernel, first, last, top_k),
+        functools.partial(unpack_kernel, group, not carry, last),
         out_shape=out_shape,
-        in_specs=[SMEM, SMEM, ANY, VMEM, VMEM, VMEM],
-        out_specs=tuple(VMEM for _ in out_shape),
-        scratch_shapes=scratch,
+        in_specs=[SMEM, SMEM, ANY, ANY] + [ANY] * len(carry),
+        out_specs=tuple(VMEM if last else ANY for _ in out_shape),
+        scratch_shapes=[
+            pltpu.VMEM((rows, height, LANES), BF16),
+            pltpu.VMEM((positions, features), BF16),
+            pltpu.VMEM((positions + 1, -(-cols // 8) * 8, LANES), F32),
+            pltpu.VMEM(acc_shape, F32),
+            pltpu.VMEM(dots_shape, F32),
+            pltpu.SemaphoreType.DMA((3 + 4,)),
+        ],
         cost_estimate=pl.CostEstimate(
             flops=8 * rows * height * LANES,
             transcendentals=0,
             bytes_accessed=rows * height * LANES * 4,
         ),
         name="unpack",
-    )(slots, weights, records, cotangent, *carry)
+    )(table, weights, records, cotangent, *carry)
 
 
 def exchange(value):
@@ -252,30 +379,19 @@
 
 def per_device(tokens, cotangent, routes, router_weights, w_gate, w_up, w_down):
     owners = lax.axis_size("cp") * lax.axis_size("ep")
-    positions = tokens.shape[1]
-    top_k = routes.shape[2]
-    count = positions * top_k
-    capacity = count // owners * 5 // 4
-    flat_routes = routes[0].reshape(count)
-    index = jnp.arange(count, dtype=jnp.int32)
-    earlier = (flat_routes[None, :] == flat_routes[:, None]) & (index[None, :] < index[:, None])
-    rank = jnp.sum(earlier.astype(jnp.int32), axis=1)
-    place = flat_routes * capacity + rank
-    holds = place[None, :] == jnp.arange(owners * capacity, dtype=jnp.int32)[:, None]
-    slot_of = count + jnp.sum(jnp.where(holds, index[None, :] - count, 0), axis=1)
-    slot_of = slot_of.reshape(owners, capacity)
-    weights = router_weights[0].reshape(count)
-
-    slots = [slot_of[:, a:b].reshape(owners * (b - a)) for a, b in GROUPS]
-    sent = [pack(s, tokens[0], cotangent[0], top_k) for s in slots]
+    tokens, cotangent = tokens[0], cotangent[0]
+    routes, weights = routes[0].T, router_weights[0].T
+
+    sent, table = first_pack(GROUPS[0], routes, tokens, cotangent, owners)
+    sent = [sent] + [next_pack(g, table, tokens, cotangent) for g in GROUPS[1:]]
     arrived = [exchange(s) for s in sent]
     done = [expert(a, w_gate[0], w_up[0], w_down[0]) for a in arrived]
     returned = [exchange(d) for d in done]
-    carry = None
-    for i, (s, r) in enumerate(zip(slots, returned)):
-        carry = unpack(s, weights, r, cotangent[0], carry, i == len(GROUPS) - 1, top_k)
+    carry = ()
+    for i, (g, r) in enumerate(zip(GROUPS, returned)):
+        carry = unpack(g, table, weights, r, cotangent, carry, i == len(GROUPS) - 1)
     layer_out, token_grad, gate_grad = carry
-    return layer_out[None], token_grad[None], gate_grad[None]
+    return layer_out[None], token_grad[None], gate_grad.T[None]
 
 
 def solution(mesh):

time: 282 us -> 275 us (0.975)
  Pallas kernels: 85.8 us -> 76.5 us
  waiting for transfers between devices: 150 us -> 159 us
  local copies, waits for them, and re-layouts: 5.44 us -> 0 us
    pallas_call x4, Pallas kernels: 34 us -> 24.5 us  [the longest x2 15.9 us: unpack(): pl.pallas_call(functools.partial(unpack_kernel, group, not carry, last),...]
    all_to_all x4, waiting for transfers between devices: 150 us -> 159 us  [exchange(): return lax.all_to_all(value, AXES, split_axis=0, concat_axis=0, tiled=True)]
  transfers between devices with their start and end apart: 4 -> 4, of which waited for: 4 -> 4; matrix products, arithmetic and copies ran while one was open for 1% -> 0% of each run, Pallas kernels for 25% -> 24%
where the time goes in v2:
time: 275 us; the launch traced here: 272 us
  waiting for transfers between devices  159 us (58%)
  Pallas kernels  76.5 us (28%)
  starting transfers between devices  35.1 us (13%)
    all_to_all x4, waiting for transfers between devices, exchange(): return lax.all_to_all(value, AXES, split_axis=0, concat_axis=0, tiled=True)  159 us
    pallas_call x2, Pallas kernels, expert(): pl.pallas_call(expert_kernel, out_shape=jax.ShapeDtypeStruct(records.shap...  52 us
    all_to_all x4, starting transfers between devices, exchange(): return lax.all_to_all(value, AXES, split_axis=0, concat_axis=0, tiled=True)  35.1 us
    pallas_call x2, Pallas kernels, unpack(): pl.pallas_call(functools.partial(unpack_kernel, group, not carry, last),...  15.9 us
  transfers between devices with their start and end apart: 4, of which 4 were waited for; matrix products, arithmetic and copies ran while one was open for 0% of the time, Pallas kernels for 24%

profile of v2, /device:TPU:34, one launch (start us, length us, event | category | flops | bytes accessed | tf_op | source)
XLA Modules:
  0.0 271.7 jit_solution(10006761721950504780)
XLA Ops:
  0.6 5.0 %first_pack.1 = (bf16[384,56,128]{2,1,0:T(8,128)(2,1)}, s32[8,128]{1,0:T(8,128)}) custom-call(s32[8,64]{1,0:T(8,128)} %bitcast.24, bf16[64,3584]{1,0:T(8,128)(2,1)} %bitcast.20, bf16[64,3584]{1,0:T(8,128)(2,1)} %bitcast.16), custom_call_target="tpu_custom_call" | custom-call | bytes 11010048 | tf_op jit(solution)/shard_map/first_pack/pallas_call | solution.py:111
  5.6 10.6 %all-to-all-start.2 = ((bf16[384,56,128]{2,1,0:T(8,128)(2,1)}), bf16[384,56,128]{2,1,0:T(8,128)(2,1)}, u32[]{:S(2)}, u32[]{:S(2)}) async-start(bf16[384,56,128]{2,1,0:T(8,128)(2,1)} %get-tuple-element.11), calls=%async_computation.2 | async-start | bytes 11010048 | tf_op jit(solution)/shard_map/all_to_all | solution.py:377
  16.2 3.6 %next_pack.1 = bf16[256,56,128]{2,1,0:T(8,128)(2,1)} custom-call(s32[8,128]{1,0:T(8,128)} %get-tuple-element.10.table, bf16[64,3584]{1,0:T(8,128)(2,1)} %bitcast.21, bf16[64,3584]{1,0:T(8,128)(2,1)} %bitcast.17), custom_call_target="tpu_custom_call" | custom-call | bytes 7340032 | tf_op jit(solution)/shard_map/next_pack/pallas_call | solution.py:138
  19.8 63.2 %all-to-all-done.2.rec_in = bf16[384,56,128]{2,1,0:T(8,128)(2,1)} async-done(((bf16[384,56,128]{2,1,0:T(8,128)(2,1)}), bf16[384,56,128]{2,1,0:T(8,128)(2,1)}, u32[]{:S(2)}, u32[]{:S(2)}) %all-to-all-start.2) | async-done | bytes 5505056 | tf_op jit(solution)/shard_map/all_to_all | solution.py:377
  83.0 8.4 %all-to-all-start = ((bf16[256,56,128]{2,1,0:T(8,128)(2,1)}), bf16[256,56,128]{2,1,0:T(8,128)(2,1)}, u32[]{:S(2)}, u32[]{:S(2)}) async-start(bf16[256,56,128]{2,1,0:T(8,128)(2,1)} %next_pack.1), calls=%async_computation | async-start | bytes 7340032 | tf_op jit(solution)/shard_map/all_to_all | solution.py:377
  91.4 29.6 %expert.3 = bf16[384,56,128]{2,1,0:T(8,128)(2,1)} custom-call(bf16[384,56,128]{2,1,0:T(8,128)(2,1)} %all-to-all-done.2.rec_in, bf16[3584,1024]{1,0:T(8,128)(2,1)} %bitcast.25, bf16[3584,1024]{1,0:T(8,128)(2,1)} %bitcast.27, bf16[1024,3584]{1,0:T(8,128)(2,1)} %bitcast.29), custom_call_target="tpu_custom_call" | custom-call | flops 16911433728 | bytes 33030144 | tf_op jit(solution)/shard_map/expert/pallas_call | solution.py:226
  121.0 15.3 %all-to-all-done.rec_in = bf16[256,56,128]{2,1,0:T(8,128)(2,1)} async-done(((bf16[256,56,128]{2,1,0:T(8,128)(2,1)}), bf16[256,56,128]{2,1,0:T(8,128)(2,1)}, u32[]{:S(2)}, u32[]{:S(2)}) %all-to-all-start) | async-done | bytes 3670048 | tf_op jit(solution)/shard_map/all_to_all | solution.py:377
  136.4 7.8 %all-to-all-start.3 = ((bf16[384,56,128]{2,1,0:T(8,128)(2,1)}), bf16[384,56,128]{2,1,0:T(8,128)(2,1)}, u32[]{:S(2)}, u32[]{:S(2)}) async-start(bf16[384,56,128]{2,1,0:T(8,128)(2,1)} %expert.3), calls=%async_computation.3 | async-start | bytes 11010048 | tf_op jit(solution)/shard_map/all_to_all | solution.py:377
  144.1 22.4 %expert.2 = bf16[256,56,128]{2,1,0:T(8,128)(2,1)} custom-call(bf16[256,56,128]{2,1,0:T(8,128)(2,1)} %all-to-all-done.rec_in, bf16[3584,1024]{1,0:T(8,128)(2,1)} %bitcast.26, bf16[3584,1024]{1,0:T(8,128)(2,1)} %bitcast.28, bf16[1024,3584]{1,0:T(8,128)(2,1)} %bitcast.30), custom_call_target="tpu_custom_call" | custom-call | flops 11274289152 | bytes 29360128 | tf_op jit(solution)/shard_map/expert/pallas_call | solution.py:226
  166.5 44.3 %all-to-all-done.3.rec_in = bf16[384,56,128]{2,1,0:T(8,128)(2,1)} async-done(((bf16[384,56,128]{2,1,0:T(8,128)(2,1)}), bf16[384,56,128]{2,1,0:T(8,128)(2,1)}, u32[]{:S(2)}, u32[]{:S(2)}) %all-to-all-start.3) | async-done | bytes 5505056 | tf_op jit(solution)/shard_map/all_to_all | solution.py:377
  210.9 8.3 %all-to-all-start.1 = ((bf16[256,56,128]{2,1,0:T(8,128)(2,1)}), bf16[256,56,128]{2,1,0:T(8,128)(2,1)}, u32[]{:S(2)}, u32[]{:S(2)}) async-start(bf16[256,56,128]{2,1,0:T(8,128)(2,1)} %expert.2), calls=%async_computation.1 | async-start | bytes 7340032 | tf_op jit(solution)/shard_map/all_to_all | solution.py:377
  219.2 8.6 %unpack.2 = (f32[65,56,128]{2,1,0:T(8,128)}, f32[584,128]{1,0:T(8,128)}) custom-call(s32[8,128]{1,0:T(8,128)} %get-tuple-element.10.table, f32[8,64]{1,0:T(8,128)} %bitcast.22, bf16[384,56,128]{2,1,0:T(8,128)(2,1)} %all-to-all-done.3.rec_in, bf16[64,3584]{1,0:T(8,128)(2,1)} %bitcast.18), custom_call_target="tpu_custom_call" | custom-call | flops 22020096 | bytes 11010048 | tf_op jit(solution)/shard_map/unpack/pallas_call | solution.py:354
  227.8 36.4 %all-to-all-done.1.rec_in = bf16[256,56,128]{2,1,0:T(8,128)(2,1)} async-done(((bf16[256,56,128]{2,1,0:T(8,128)(2,1)}), bf16[256,56,128]{2,1,0:T(8,128)(2,1)}, u32[]{:S(2)}, u32[]{:S(2)}) %all-to-all-start.1) | async-done | bytes 3670048 | tf_op jit(solution)/shard_map/all_to_all | solution.py:377
  264.2 7.3 %unpack.3 = (bf16[64,3584]{1,0:T(8,128)(2,1)}, bf16[64,3584]{1,0:T(8,128)(2,1)}, f32[8,64]{1,0:T(8,128)}) custom-call(s32[8,128]{1,0:T(8,128)} %get-tuple-element.10.table, f32[8,64]{1,0:T(8,128)} %bitcast.23, bf16[256,56,128]{2,1,0:T(8,128)(2,1)} %all-to-all-done.1.rec_in, bf16[64,3584]{1,0:T(8,128)(2,1)} %bitcast.19, ...), custom_call_target="tpu_custom_call" | custom-call | flops 14680064 | bytes 7340032 | tf_op jit(solution)/shard_map/unpack/pallas_call | solution.py:354
Async XLA Ops:
  5.6 77.4 %all-to-all-start.2 = ((bf16[384,56,128]{2,1,0:T(8,128)(2,1)}), bf16[384,56,128]{2,1,0:T(8,128)(2,1)}, u32[]{:S(2)}, u32[]{:S(2)}) async-start(bf16[384,56,128]{2,1,0:T(8,128)(2,1)} %get-tuple-element.11), calls=%async_computation.2 | async-start | bytes 11010048 | tf_op jit(solution)/shard_map/all_to_all | solution.py:377
  83.0 53.4 %all-to-all-start = ((bf16[256,56,128]{2,1,0:T(8,128)(2,1)}), bf16[256,56,128]{2,1,0:T(8,128)(2,1)}, u32[]{:S(2)}, u32[]{:S(2)}) async-start(bf16[256,56,128]{2,1,0:T(8,128)(2,1)} %next_pack.1), calls=%async_computation | async-start | bytes 7340032 | tf_op jit(solution)/shard_map/all_to_all | solution.py:377
  136.4 74.5 %all-to-all-start.3 = ((bf16[384,56,128]{2,1,0:T(8,128)(2,1)}), bf16[384,56,128]{2,1,0:T(8,128)(2,1)}, u32[]{:S(2)}, u32[]{:S(2)}) async-start(bf16[384,56,128]{2,1,0:T(8,128)(2,1)} %expert.3), calls=%async_computation.3 | async-start | bytes 11010048 | tf_op jit(solution)/shard_map/all_to_all | solution.py:377
  210.9 53.3 %all-to-all-start.1 = ((bf16[256,56,128]{2,1,0:T(8,128)(2,1)}), bf16[256,56,128]{2,1,0:T(8,128)(2,1)}, u32[]{:S(2)}, u32[]{:S(2)}) async-start(bf16[256,56,128]{2,1,0:T(8,128)(2,1)} %expert.2), calls=%async_computation.1 | async-start | bytes 7340032 | tf_op jit(solution)/shard_map/all_to_all | solution.py:377

commit v3 on v2

--- a/solution.py
+++ b/solution.py
@@ -8,6 +8,8 @@
 from jax.sharding import PartitionSpec as P
 
 LANES = 128
+CHUNKS = 8
+UNROLL = 2
 GROUPS = ((0, 3), (3, 5))
 AXES = ("cp", "ep")
 SPAN = 128
@@ -68,29 +70,32 @@
 
 
 def first_pack_kernel(
-    group, routes, tokens_in, cotangent_in, out, table_out,
-    tokens, cotangent, table, table_smem, flat, records, sem, sems,
+    group, routes_in, tokens_in, cotangent_in, out, table_out,
+    routes, tokens, cotangent, table, table_smem, flat, records, sem, sems,
 ):
     positions = tokens.shape[0]
     load = [
-        pltpu.make_async_copy(tokens_in, tokens, sems.at[0]),
-        pltpu.make_async_copy(cotangent_in, cotangent, sems.at[1]),
+        pltpu.make_async_copy(src, dst, sems.at[i])
+        for i, (src, dst) in enumerate(
+            ((routes_in, routes), (tokens_in, tokens), (cotangent_in, cotangent))
+        )
     ]
     for c in load:
         c.start()
+    load[0].wait()
     table[...] = route(routes, positions, table.shape[1])
     keep = [
-        pltpu.make_async_copy(table, table_smem, sems.at[2]),
-        pltpu.make_async_copy(table, table_out, sems.at[3]),
+        pltpu.make_async_copy(table, table_smem, sems.at[3]),
+        pltpu.make_async_copy(table, table_out, sems.at[4]),
     ]
     for c in keep:
         c.start()
-    for c in load:
+    for c in load[1:]:
         c.wait()
     build_records(tokens, cotangent, flat, records)
-    for c in keep:
-        c.wait()
+    keep[0].wait()
     send_records(group, table_smem, records, out, sem)
+    keep[1].wait()
 
 
 def next_pack_kernel(group, table, tokens, cotangent, out, flat, records, sem):
@@ -114,9 +119,10 @@
             jax.ShapeDtypeStruct((rows, height, LANES), BF16),
             jax.ShapeDtypeStruct((8, owners), jnp.int32),
         ),
-        in_specs=[VMEM, ANY, ANY],
+        in_specs=[ANY, ANY, ANY],
         out_specs=(ANY, ANY),
         scratch_shapes=[
+            pltpu.VMEM(routes.shape, jnp.int32),
             pltpu.VMEM((positions, features), BF16),
             pltpu.VMEM((positions, features), BF16),
             pltpu.VMEM((8, owners), jnp.int32),
@@ -124,7 +130,7 @@
             pltpu.VMEM((positions * height, LANES), F32),
             pltpu.VMEM((positions + 1, height, LANES), BF16),
             pltpu.SemaphoreType.DMA,
-            pltpu.SemaphoreType.DMA((4,)),
+            pltpu.SemaphoreType.DMA((5,)),
         ],
         cost_estimate=pack_cost(rows, height),
         name="first_pack",
@@ -251,47 +257,62 @@
     )(records, w_gate, w_up, w_down)
 
 
-def unpack_kernel(group, first, last, table, weights, rec_in, cotangent_in, *rest):
+def unpack_kernel(group, first, last, table_in, weights_in, rec_in, cotangent_in, *rest):
     if not first:
-        acc_in, dots_in, *rest = rest
+        acc_in, dots_in, cot_in, *rest = rest
     if last:
-        layer_out, token_grad, gate_grad, *rest = rest
+        layer_to, grad_to, gate_to, *rest = rest
     else:
-        acc_out, dots_out, *rest = rest
-    rec, cotangent, cot, acc, dots, sems = rest
+        acc_out, dots_out, cot_out, *rest = rest
+    (
+        table, weights, rec, cotangent, cot, dots, sems, layer_out, token_grad, gate_grad, old_dots, *accs
+    ) = rest
+    acc = accs[0]
     positions, features = cotangent.shape
     rows, height, _ = rec.shape
     top_k = weights.shape[0]
     cols = features // LANES
-    chunks = sems.shape[0] - 3
+    chunks = sems.shape[0] - 5
     part = rows // chunks
     loads = [
         pltpu.make_async_copy(
-            rec_in.at[pl.ds(c * part, part)], rec.at[pl.ds(c * part, part)], sems.at[3 + c]
+            rec_in.at[pl.ds(c * part, part)], rec.at[pl.ds(c * part, part)], sems.at[5 + c]
         )
         for c in range(chunks)
     ]
-    others = [pltpu.make_async_copy(cotangent_in, cotangent, sems.at[0])]
-    if not first:
-        others.append(pltpu.make_async_copy(acc_in, acc, sems.at[1]))
-        others.append(pltpu.make_async_copy(dots_in, dots, sems.at[2]))
-    for c in others[:1] + loads[:1] + others[1:] + loads[1:]:
+    tall = cot.shape[1]
+    if first:
+        others = [pltpu.make_async_copy(cotangent_in, cotangent, sems.at[0])]
+    else:
+        others = [
+            pltpu.make_async_copy(src, dst, sems.at[i])
+            for i, (src, dst) in enumerate(
+                ((cot_in, cot), (acc_in, accs[1]), (dots_in, old_dots))
+            )
+        ]
+    small = [
+        pltpu.make_async_copy(table_in, table, sems.at[3]),
+        pltpu.make_async_copy(weights_in, weights, sems.at[4]),
+    ]
+    for c in small + others[:1] + loads + others[1:]:
         c.start()
+    acc[...] = jnp.zeros_like(acc)
+    dots[...] = jnp.zeros_like(dots)
     if first:
-        acc[...] = jnp.zeros_like(acc)
-        dots[...] = jnp.zeros_like(dots)
-    cot[...] = jnp.zeros_like(cot)
-    tall = cot.shape[1]
-    flat_cot = cot.reshape(cot.shape[0] * tall, LANES)
-    others[0].wait()
-    for j in range(cols):
-        flat_cot[pl.ds(j, positions, stride=tall), :] = cotangent[
-            :, j * LANES : (j + 1) * LANES
-        ].astype(F32)
-    for c in others[1:]:
+        cot[...] = jnp.zeros_like(cot)
+        flat_cot = cot.reshape(cot.shape[0] * tall, LANES)
+        others[0].wait()
+        for j in range(cols):
+            flat_cot[pl.ds(j, positions, stride=tall), :] = cotangent[
+                :, j * LANES : (j + 1) * LANES
+            ].astype(F32)
+    else:
+        others[0].wait()
+    for c in small:
         c.wait()
     span = group[1] - group[0]
-    together = 2 * span
+    experts = UNROLL
+    together = experts * span
 
     for c in range(chunks):
         loads[c].wait()
@@ -301,7 +322,7 @@
             todo = []
             for u in range(together):
                 r = c * part + step * together + u
-                expert_at = c * (part // span) + step * 2 + u // span
+                expert_at = c * (part // span) + step * experts + u // span
                 slot = table[group[0] + u % span, expert_at]
                 token = slot & (SPAN - 1)
                 k = slot // SPAN
@@ -309,21 +330,34 @@
                 value = rec[r].astype(F32)
                 dot = jnp.sum(cot[token] * value[:tall], axis=0, keepdims=True)
                 todo.append((token, k * positions + token, weight * value, dot))
-            for token, at, scaled, dot in todo:
+            for u, (token, at, scaled, dot) in enumerate(todo):
                 acc[token] += scaled
                 dots[pl.ds(at, 1), :] = dot
 
     if last:
-        gate_grad[...] = jnp.sum(
-            dots[0 : top_k * positions].reshape(top_k, positions, LANES), axis=2
-        )
-        flat = acc.reshape((positions + 1) * height, LANES)
-        for j in range(cols):
-            lanes = slice(j * LANES, (j + 1) * LANES)
-            layer_out[:, lanes] = flat[pl.ds(j, positions, stride=height), :].astype(BF16)
-            token_grad[:, lanes] = flat[pl.ds(cols + j, positions, stride=height), :].astype(BF16)
+        for c in others[1:]:
+            c.wait()
+        stores = [
+            pltpu.make_async_copy(src, dst, sems.at[i])
+            for i, (src, dst) in enumerate(
+                ((layer_out, layer_to), (token_grad, grad_to), (gate_grad, gate_to))
+            )
+        ]
+        flats = [a.reshape((positions + 1) * height, LANES) for a in accs]
+        for at, out in enumerate((layer_out, token_grad)):
+            for j in range(cols):
+                rows_at = pl.ds(at * cols + j, positions, stride=height)
+                total = sum((f[rows_at, :] for f in flats[1:]), flats[0][rows_at, :])
+                out[:, j * LANES : (j + 1) * LANES] = total.astype(BF16)
+            stores[at].start()
+        both = dots[0 : top_k * positions] + old_dots[0 : top_k * positions]
+        gate_grad[...] = jnp.sum(both.reshape(top_k, positions, LANES), axis=2)
+        stores[2].start()
+        for c in stores:
+            c.wait()
     else:
         stores = [
+            pltpu.make_async_copy(cot, cot_out, sems.at[0]),
             pltpu.make_async_copy(acc, acc_out, sems.at[1]),
             pltpu.make_async_copy(dots, dots_out, sems.at[2]),
         ]
@@ -339,6 +373,7 @@
     top_k = weights.shape[0]
     cols = features // LANES
     acc_shape = (positions + 1, height, LANES)
+    cot_shape = (positions + 1, -(-cols // 8) * 8, LANES)
     dots_shape = (top_k * positions + positions + 8, LANES)
     if last:
         out_shape = (
@@ -350,20 +385,28 @@
         out_shape = (
             jax.ShapeDtypeStruct(acc_shape, F32),
             jax.ShapeDtypeStruct(dots_shape, F32),
+            jax.ShapeDtypeStruct(cot_shape, F32),
         )
     return pl.pallas_call(
         functools.partial(unpack_kernel, group, not carry, last),
         out_shape=out_shape,
-        in_specs=[SMEM, SMEM, ANY, ANY] + [ANY] * len(carry),
-        out_specs=tuple(VMEM if last else ANY for _ in out_shape),
+        in_specs=[ANY] * (4 + len(carry)),
+        out_specs=tuple(ANY for _ in out_shape),
         scratch_shapes=[
+            pltpu.SMEM(table.shape, jnp.int32),
+            pltpu.SMEM(weights.shape, F32),
             pltpu.VMEM((rows, height, LANES), BF16),
             pltpu.VMEM((positions, features), BF16),
-            pltpu.VMEM((positions + 1, -(-cols // 8) * 8, LANES), F32),
+            pltpu.VMEM(cot_shape, F32),
+            pltpu.VMEM(dots_shape, F32),
+            pltpu.SemaphoreType.DMA((5 + CHUNKS,)),
+            pltpu.VMEM((positions, features), BF16),
+            pltpu.VMEM((positions, features), BF16),
+            pltpu.VMEM((top_k, positions), F32),
+            pltpu.VMEM(dots_shape, F32),
             pltpu.VMEM(acc_shape, F32),
-            pltpu.VMEM(dots_shape, F32),
-            pltpu.SemaphoreType.DMA((3 + 4,)),
-        ],
+        ]
+        + [pltpu.VMEM(acc_shape, F32)] * bool(carry),
         cost_estimate=pl.CostEstimate(
             flops=8 * rows * height * LANES,
             transcendentals=0,

time: 275 us -> 274 us (level)
  no operation moved by 1% of the time
where the time goes in v3:
time: 274 us; the launch traced here: 270 us
  waiting for transfers between devices  160 us (58%)
  Pallas kernels  74.4 us (27%)
  starting transfers between devices  35.1 us (13%)
    all_to_all x4, waiting for transfers between devices, exchange(): return lax.all_to_all(value, AXES, split_axis=0, concat_axis=0, tiled=True)  160 us
    pallas_call x2, Pallas kernels, expert(): pl.pallas_call(expert_kernel, out_shape=jax.ShapeDtypeStruct(records.shap...  52 us
    all_to_all x4, starting transfers between devices, exchange(): return lax.all_to_all(value, AXES, split_axis=0, concat_axis=0, tiled=True)  35.1 us
    pallas_call x2, Pallas kernels, unpack(): pl.pallas_call(functools.partial(unpack_kernel, group, not carry, last),...  14.4 us
  transfers between devices with their start and end apart: 4, of which 4 were waited for; matrix products, arithmetic and copies ran while one was open for 0% of the time, Pallas kernels for 24%

profile of v3, /device:TPU:34, one launch (start us, length us, event | category | flops | bytes accessed | tf_op | source)
XLA Modules:
  0.0 270.1 jit_solution(14366595349491145931)
XLA Ops:
  0.6 4.4 %first_pack.1 = (bf16[384,56,128]{2,1,0:T(8,128)(2,1)}, s32[8,128]{1,0:T(8,128)}) custom-call(s32[8,64]{1,0:T(8,128)} %bitcast.24, bf16[64,3584]{1,0:T(8,128)(2,1)} %bitcast.20, bf16[64,3584]{1,0:T(8,128)(2,1)} %bitcast.16), custom_call_target="tpu_custom_call" | custom-call | bytes 11010048 | tf_op jit(solution)/shard_map/first_pack/pallas_call | solution.py:116
  5.0 10.6 %all-to-all-start.2 = ((bf16[384,56,128]{2,1,0:T(8,128)(2,1)}), bf16[384,56,128]{2,1,0:T(8,128)(2,1)}, u32[]{:S(2)}, u32[]{:S(2)}) async-start(bf16[384,56,128]{2,1,0:T(8,128)(2,1)} %get-tuple-element.12), calls=%async_computation.2 | async-start | bytes 11010048 | tf_op jit(solution)/shard_map/all_to_all | solution.py:420
  15.6 3.6 %next_pack.1 = bf16[256,56,128]{2,1,0:T(8,128)(2,1)} custom-call(s32[8,128]{1,0:T(8,128)} %get-tuple-element.11.table.table_in, bf16[64,3584]{1,0:T(8,128)(2,1)} %bitcast.21, bf16[64,3584]{1,0:T(8,128)(2,1)} %bitcast.17), custom_call_target="tpu_custom_call" | custom-call | bytes 7340032 | tf_op jit(solution)/shard_map/next_pack/pallas_call | solution.py:144
  19.2 63.2 %all-to-all-done.2.rec_in = bf16[384,56,128]{2,1,0:T(8,128)(2,1)} async-done(((bf16[384,56,128]{2,1,0:T(8,128)(2,1)}), bf16[384,56,128]{2,1,0:T(8,128)(2,1)}, u32[]{:S(2)}, u32[]{:S(2)}) %all-to-all-start.2) | async-done | bytes 5505056 | tf_op jit(solution)/shard_map/all_to_all | solution.py:420
  82.4 8.4 %all-to-all-start = ((bf16[256,56,128]{2,1,0:T(8,128)(2,1)}), bf16[256,56,128]{2,1,0:T(8,128)(2,1)}, u32[]{:S(2)}, u32[]{:S(2)}) async-start(bf16[256,56,128]{2,1,0:T(8,128)(2,1)} %next_pack.1), calls=%async_computation | async-start | bytes 7340032 | tf_op jit(solution)/shard_map/all_to_all | solution.py:420
  90.8 29.6 %expert.3 = bf16[384,56,128]{2,1,0:T(8,128)(2,1)} custom-call(bf16[384,56,128]{2,1,0:T(8,128)(2,1)} %all-to-all-done.2.rec_in, bf16[3584,1024]{1,0:T(8,128)(2,1)} %bitcast.25, bf16[3584,1024]{1,0:T(8,128)(2,1)} %bitcast.27, bf16[1024,3584]{1,0:T(8,128)(2,1)} %bitcast.29), custom_call_target="tpu_custom_call" | custom-call | flops 16911433728 | bytes 33030144 | tf_op jit(solution)/shard_map/expert/pallas_call | solution.py:232
  120.4 15.3 %all-to-all-done.rec_in = bf16[256,56,128]{2,1,0:T(8,128)(2,1)} async-done(((bf16[256,56,128]{2,1,0:T(8,128)(2,1)}), bf16[256,56,128]{2,1,0:T(8,128)(2,1)}, u32[]{:S(2)}, u32[]{:S(2)}) %all-to-all-start) | async-done | bytes 3670048 | tf_op jit(solution)/shard_map/all_to_all | solution.py:420
  135.7 7.8 %all-to-all-start.3 = ((bf16[384,56,128]{2,1,0:T(8,128)(2,1)}), bf16[384,56,128]{2,1,0:T(8,128)(2,1)}, u32[]{:S(2)}, u32[]{:S(2)}) async-start(bf16[384,56,128]{2,1,0:T(8,128)(2,1)} %expert.3), calls=%async_computation.3 | async-start | bytes 11010048 | tf_op jit(solution)/shard_map/all_to_all | solution.py:420
  143.5 22.4 %expert.2 = bf16[256,56,128]{2,1,0:T(8,128)(2,1)} custom-call(bf16[256,56,128]{2,1,0:T(8,128)(2,1)} %all-to-all-done.rec_in, bf16[3584,1024]{1,0:T(8,128)(2,1)} %bitcast.26, bf16[3584,1024]{1,0:T(8,128)(2,1)} %bitcast.28, bf16[1024,3584]{1,0:T(8,128)(2,1)} %bitcast.30), custom_call_target="tpu_custom_call" | custom-call | flops 11274289152 | bytes 29360128 | tf_op jit(solution)/shard_map/expert/pallas_call | solution.py:232
  165.9 44.3 %all-to-all-done.3.rec_in = bf16[384,56,128]{2,1,0:T(8,128)(2,1)} async-done(((bf16[384,56,128]{2,1,0:T(8,128)(2,1)}), bf16[384,56,128]{2,1,0:T(8,128)(2,1)}, u32[]{:S(2)}, u32[]{:S(2)}) %all-to-all-start.3) | async-done | bytes 5505056 | tf_op jit(solution)/shard_map/all_to_all | solution.py:420
  210.2 8.4 %all-to-all-start.1 = ((bf16[256,56,128]{2,1,0:T(8,128)(2,1)}), bf16[256,56,128]{2,1,0:T(8,128)(2,1)}, u32[]{:S(2)}, u32[]{:S(2)}) async-start(bf16[256,56,128]{2,1,0:T(8,128)(2,1)} %expert.2), calls=%async_computation.1 | async-start | bytes 7340032 | tf_op jit(solution)/shard_map/all_to_all | solution.py:420
  218.6 8.2 %unpack.2 = (f32[65,56,128]{2,1,0:T(8,128)}, f32[584,128]{1,0:T(8,128)}, f32[65,32,128]{2,1,0:T(8,128)}) custom-call(s32[8,128]{1,0:T(8,128)} %get-tuple-element.11.table.table_in, f32[8,64]{1,0:T(8,128)} %bitcast.22, bf16[384,56,128]{2,1,0:T(8,128)(2,1)} %all-to-all-done.3.rec_in, bf16[64,3584]{1,0:T(8,128)(2,1)} %bitcast.18), custom_call_target="tpu_custom_call" | custom-call | flops 22020096 | bytes 11010048 | tf_op jit(solution)/shard_map/unpack/pallas_call | solution.py:390
  226.8 36.8 %all-to-all-done.1.rec_in = bf16[256,56,128]{2,1,0:T(8,128)(2,1)} async-done(((bf16[256,56,128]{2,1,0:T(8,128)(2,1)}), bf16[256,56,128]{2,1,0:T(8,128)(2,1)}, u32[]{:S(2)}, u32[]{:S(2)}) %all-to-all-start.1) | async-done | bytes 3670048 | tf_op jit(solution)/shard_map/all_to_all | solution.py:420
  263.6 6.3 %unpack.3 = (bf16[64,3584]{1,0:T(8,128)(2,1)}, bf16[64,3584]{1,0:T(8,128)(2,1)}, f32[8,64]{1,0:T(8,128)}) custom-call(s32[8,128]{1,0:T(8,128)} %get-tuple-element.11.table.table_in, f32[8,64]{1,0:T(8,128)} %bitcast.23, bf16[256,56,128]{2,1,0:T(8,128)(2,1)} %all-to-all-done.1.rec_in, bf16[64,3584]{1,0:T(8,128)(2,1)} %bitcast.19, ...), custom_call_target="tpu_custom_call" | custom-call | flops 14680064 | bytes 7340032 | tf_op jit(solution)/shard_map/unpack/pallas_call | solution.py:390
Async XLA Ops:
  5.0 77.4 %all-to-all-start.2 = ((bf16[384,56,128]{2,1,0:T(8,128)(2,1)}), bf16[384,56,128]{2,1,0:T(8,128)(2,1)}, u32[]{:S(2)}, u32[]{:S(2)}) async-start(bf16[384,56,128]{2,1,0:T(8,128)(2,1)} %get-tuple-element.12), calls=%async_computation.2 | async-start | bytes 11010048 | tf_op jit(solution)/shard_map/all_to_all | solution.py:420
  82.4 53.4 %all-to-all-start = ((bf16[256,56,128]{2,1,0:T(8,128)(2,1)}), bf16[256,56,128]{2,1,0:T(8,128)(2,1)}, u32[]{:S(2)}, u32[]{:S(2)}) async-start(bf16[256,56,128]{2,1,0:T(8,128)(2,1)} %next_pack.1), calls=%async_computation | async-start | bytes 7340032 | tf_op jit(solution)/shard_map/all_to_all | solution.py:420
  135.7 74.5 %all-to-all-start.3 = ((bf16[384,56,128]{2,1,0:T(8,128)(2,1)}), bf16[384,56,128]{2,1,0:T(8,128)(2,1)}, u32[]{:S(2)}, u32[]{:S(2)}) async-start(bf16[384,56,128]{2,1,0:T(8,128)(2,1)} %expert.3), calls=%async_computation.3 | async-start | bytes 11010048 | tf_op jit(solution)/shard_map/all_to_all | solution.py:420
  210.2 53.3 %all-to-all-start.1 = ((bf16[256,56,128]{2,1,0:T(8,128)(2,1)}), bf16[256,56,128]{2,1,0:T(8,128)(2,1)}, u32[]{:S(2)}, u32[]{:S(2)}) async-start(bf16[256,56,128]{2,1,0:T(8,128)(2,1)} %expert.2), calls=%async_computation.1 | async-start | bytes 7340032 | tf_op jit(solution)/shard_map/all_to_all | solution.py:420

commit v4 on v3

--- a/solution.py
+++ b/solution.py
@@ -9,6 +9,7 @@
 
 LANES = 128
 CHUNKS = 8
+PIECES = 4
 UNROLL = 2
 GROUPS = ((0, 3), (3, 5))
 AXES = ("cp", "ep")
@@ -258,41 +259,34 @@
 
 
 def unpack_kernel(group, first, last, table_in, weights_in, rec_in, cotangent_in, *rest):
-    if not first:
-        acc_in, dots_in, cot_in, *rest = rest
-    if last:
-        layer_to, grad_to, gate_to, *rest = rest
-    else:
-        acc_out, dots_out, cot_out, *rest = rest
-    (
-        table, weights, rec, cotangent, cot, dots, sems, layer_out, token_grad, gate_grad, old_dots, *accs
-    ) = rest
-    acc = accs[0]
+    kept = 0 if first else 4
+    carry_in, rest = rest[:kept], rest[kept:]
+    sent = 3 if last else 4
+    outs, rest = rest[:sent], rest[sent:]
+    table, weights, rec, cotangent, cot, acc, dots, sems, *rest = rest
+    results, old = rest[:3], rest[3:]
     positions, features = cotangent.shape
     rows, height, _ = rec.shape
     top_k = weights.shape[0]
     cols = features // LANES
-    chunks = sems.shape[0] - 5
-    part = rows // chunks
+    tall = cot.shape[1]
+    part = rows // CHUNKS
     loads = [
         pltpu.make_async_copy(
-            rec_in.at[pl.ds(c * part, part)], rec.at[pl.ds(c * part, part)], sems.at[5 + c]
+            rec_in.at[pl.ds(c * part, part)], rec.at[pl.ds(c * part, part)], sems.at[6 + c]
         )
-        for c in range(chunks)
-    ]
-    tall = cot.shape[1]
+        for c in range(CHUNKS)
+    ]
     if first:
         others = [pltpu.make_async_copy(cotangent_in, cotangent, sems.at[0])]
     else:
         others = [
             pltpu.make_async_copy(src, dst, sems.at[i])
-            for i, (src, dst) in enumerate(
-                ((cot_in, cot), (acc_in, accs[1]), (dots_in, old_dots))
-            )
+            for i, (src, dst) in enumerate(zip(carry_in, (cot, *old)))
         ]
     small = [
-        pltpu.make_async_copy(table_in, table, sems.at[3]),
-        pltpu.make_async_copy(weights_in, weights, sems.at[4]),
+        pltpu.make_async_copy(table_in, table, sems.at[4]),
+        pltpu.make_async_copy(weights_in, weights, sems.at[5]),
     ]
     for c in small + others[:1] + loads + others[1:]:
         c.start()
@@ -311,10 +305,9 @@
     for c in small:
         c.wait()
     span = group[1] - group[0]
-    experts = UNROLL
-    together = experts * span
-
-    for c in range(chunks):
+    together = UNROLL * span
+
+    for c in range(CHUNKS):
         loads[c].wait()
 
         @pl.loop(0, part // together)
@@ -322,7 +315,7 @@
             todo = []
             for u in range(together):
                 r = c * part + step * together + u
-                expert_at = c * (part // span) + step * experts + u // span
+                expert_at = c * (part // span) + step * UNROLL + u // span
                 slot = table[group[0] + u % span, expert_at]
                 token = slot & (SPAN - 1)
                 k = slot // SPAN
@@ -330,41 +323,40 @@
                 value = rec[r].astype(F32)
                 dot = jnp.sum(cot[token] * value[:tall], axis=0, keepdims=True)
                 todo.append((token, k * positions + token, weight * value, dot))
-            for u, (token, at, scaled, dot) in enumerate(todo):
+            for token, at, scaled, dot in todo:
                 acc[token] += scaled
                 dots[pl.ds(at, 1), :] = dot
 
-    if last:
-        for c in others[1:]:
-            c.wait()
-        stores = [
-            pltpu.make_async_copy(src, dst, sems.at[i])
-            for i, (src, dst) in enumerate(
-                ((layer_out, layer_to), (token_grad, grad_to), (gate_grad, gate_to))
+    for c in others[1:]:
+        c.wait()
+    flat = acc.reshape((positions + 1) * height, LANES)
+    piece = cols // PIECES
+    stores = []
+    for at in range(2):
+        for p in range(PIECES):
+            for j in range(p * piece, (p + 1) * piece):
+                lanes = slice(j * LANES, (j + 1) * LANES)
+                total = flat[pl.ds(at * cols + j, positions, stride=height), :]
+                if not first:
+                    total = total + old[at][:, lanes]
+                results[at][:, lanes] = total.astype(results[at].dtype)
+            lanes = pl.ds(p * piece * LANES, piece * LANES)
+            store = pltpu.make_async_copy(
+                results[at].at[:, lanes], outs[at + sent - 3].at[:, lanes], sems.at[6 + len(stores)]
             )
-        ]
-        flats = [a.reshape((positions + 1) * height, LANES) for a in accs]
-        for at, out in enumerate((layer_out, token_grad)):
-            for j in range(cols):
-                rows_at = pl.ds(at * cols + j, positions, stride=height)
-                total = sum((f[rows_at, :] for f in flats[1:]), flats[0][rows_at, :])
-                out[:, j * LANES : (j + 1) * LANES] = total.astype(BF16)
-            stores[at].start()
-        both = dots[0 : top_k * positions] + old_dots[0 : top_k * positions]
-        gate_grad[...] = jnp.sum(both.reshape(top_k, positions, LANES), axis=2)
-        stores[2].start()
-        for c in stores:
-            c.wait()
-    else:
-        stores = [
-            pltpu.make_async_copy(cot, cot_out, sems.at[0]),
-            pltpu.make_async_copy(acc, acc_out, sems.at[1]),
-            pltpu.make_async_copy(dots, dots_out, sems.at[2]),
-        ]
-        for c in stores:
-            c.start()
-        for c in stores:
-            c.wait()
+            store.start()
+            stores.append(store)
+    total = jnp.sum(dots[0 : top_k * positions].reshape(top_k, positions, LANES), axis=2)
+    if not first:
+        total = total + old[2][...]
+    results[2][...] = total
+    stores.append(pltpu.make_async_copy(results[2], outs[-1], sems.at[5]))
+    stores[-1].start()
+    if not last:
+        stores.append(pltpu.make_async_copy(cot, outs[0], sems.at[4]))
+        stores[-1].start()
+    for c in stores:
+        c.wait()
 
 
 def unpack(group, table, weights, records, cotangent, carry, last):
@@ -372,41 +364,29 @@
     rows, height, _ = records.shape
     top_k = weights.shape[0]
     cols = features // LANES
-    acc_shape = (positions + 1, height, LANES)
     cot_shape = (positions + 1, -(-cols // 8) * 8, LANES)
-    dots_shape = (top_k * positions + positions + 8, LANES)
-    if last:
-        out_shape = (
-            jax.ShapeDtypeStruct((positions, features), BF16),
-            jax.ShapeDtypeStruct((positions, features), BF16),
-            jax.ShapeDtypeStruct((top_k, positions), F32),
-        )
-    else:
-        out_shape = (
-            jax.ShapeDtypeStruct(acc_shape, F32),
-            jax.ShapeDtypeStruct(dots_shape, F32),
-            jax.ShapeDtypeStruct(cot_shape, F32),
-        )
+    kind = BF16 if last else F32
+    results = [
+        ((positions, features), kind), ((positions, features), kind), ((top_k, positions), F32)
+    ]
+    sent = results if last else [(cot_shape, F32)] + results
     return pl.pallas_call(
         functools.partial(unpack_kernel, group, not carry, last),
-        out_shape=out_shape,
+        out_shape=tuple(jax.ShapeDtypeStruct(*r) for r in sent),
         in_specs=[ANY] * (4 + len(carry)),
-        out_specs=tuple(ANY for _ in out_shape),
+        out_specs=tuple(ANY for _ in sent),
         scratch_shapes=[
             pltpu.SMEM(table.shape, jnp.int32),
             pltpu.SMEM(weights.shape, F32),
             pltpu.VMEM((rows, height, LANES), BF16),
             pltpu.VMEM((positions, features), BF16),
             pltpu.VMEM(cot_shape, F32),
-            pltpu.VMEM(dots_shape, F32),
-            pltpu.SemaphoreType.DMA((5 + CHUNKS,)),
-            pltpu.VMEM((positions, features), BF16),
-            pltpu.VMEM((positions, features), BF16),
-            pltpu.VMEM((top_k, positions), F32),
-            pltpu.VMEM(dots_shape, F32),
-            pltpu.VMEM(acc_shape, F32),
+            pltpu.VMEM((positions + 1, height, LANES), F32),
+            pltpu.VMEM((top_k * positions + positions + 8, LANES), F32),
+            pltpu.SemaphoreType.DMA((6 + CHUNKS,)),
         ]
-        + [pltpu.VMEM(acc_shape, F32)] * bool(carry),
+        + [pltpu.VMEM(*r) for r in results]
+        + [pltpu.VMEM(shape, F32) for shape, _ in results if carry],
         cost_estimate=pl.CostEstimate(
             flops=8 * rows * height * LANES,
             transcendentals=0,

time: 274 us -> 273 us (level)
  no operation moved by 1% of the time
where the time goes in v4:
time: 273 us; the launch traced here: 270 us
  waiting for transfers between devices  160 us (59%)
  Pallas kernels  74.1 us (27%)
  starting transfers between devices  35.1 us (13%)
    all_to_all x4, waiting for transfers between devices, exchange(): return lax.all_to_all(value, AXES, split_axis=0, concat_axis=0, tiled=True)  160 us
    pallas_call x2, Pallas kernels, expert(): pl.pallas_call(expert_kernel, out_shape=jax.ShapeDtypeStruct(records.shap...  52 us
    all_to_all x4, starting transfers between devices, exchange(): return lax.all_to_all(value, AXES, split_axis=0, concat_axis=0, tiled=True)  35.1 us
    pallas_call x2, Pallas kernels, unpack(): pl.pallas_call(functools.partial(unpack_kernel, group, not carry, last),...  14.2 us
  transfers between devices with their start and end apart: 4, of which 4 were waited for; matrix products, arithmetic and copies ran while one was open for 0% of the time, Pallas kernels for 24%

profile of v4, /device:TPU:34, one launch (start us, length us, event | category | flops | bytes accessed | tf_op | source)
XLA Modules:
  0.0 269.7 jit_solution(16743752211329697282)
XLA Ops:
  0.6 4.4 %first_pack.1 = (bf16[384,56,128]{2,1,0:T(8,128)(2,1)}, s32[8,128]{1,0:T(8,128)}) custom-call(s32[8,64]{1,0:T(8,128)} %bitcast.24, bf16[64,3584]{1,0:T(8,128)(2,1)} %bitcast.20, bf16[64,3584]{1,0:T(8,128)(2,1)} %bitcast.16), custom_call_target="tpu_custom_call" | custom-call | bytes 11010048 | tf_op jit(solution)/shard_map/first_pack/pallas_call | solution.py:117
  5.0 10.6 %all-to-all-start.2 = ((bf16[384,56,128]{2,1,0:T(8,128)(2,1)}), bf16[384,56,128]{2,1,0:T(8,128)(2,1)}, u32[]{:S(2)}, u32[]{:S(2)}) async-start(bf16[384,56,128]{2,1,0:T(8,128)(2,1)} %get-tuple-element.13), calls=%async_computation.2 | async-start | bytes 11010048 | tf_op jit(solution)/shard_map/all_to_all | solution.py:400
  15.6 3.6 %next_pack.1 = bf16[256,56,128]{2,1,0:T(8,128)(2,1)} custom-call(s32[8,128]{1,0:T(8,128)} %get-tuple-element.12.table.table_in, bf16[64,3584]{1,0:T(8,128)(2,1)} %bitcast.21, bf16[64,3584]{1,0:T(8,128)(2,1)} %bitcast.17), custom_call_target="tpu_custom_call" | custom-call | bytes 7340032 | tf_op jit(solution)/shard_map/next_pack/pallas_call | solution.py:145
  19.2 63.2 %all-to-all-done.2.rec_in = bf16[384,56,128]{2,1,0:T(8,128)(2,1)} async-done(((bf16[384,56,128]{2,1,0:T(8,128)(2,1)}), bf16[384,56,128]{2,1,0:T(8,128)(2,1)}, u32[]{:S(2)}, u32[]{:S(2)}) %all-to-all-start.2) | async-done | bytes 5505056 | tf_op jit(solution)/shard_map/all_to_all | solution.py:400
  82.4 8.4 %all-to-all-start = ((bf16[256,56,128]{2,1,0:T(8,128)(2,1)}), bf16[256,56,128]{2,1,0:T(8,128)(2,1)}, u32[]{:S(2)}, u32[]{:S(2)}) async-start(bf16[256,56,128]{2,1,0:T(8,128)(2,1)} %next_pack.1), calls=%async_computation | async-start | bytes 7340032 | tf_op jit(solution)/shard_map/all_to_all | solution.py:400
  90.8 29.6 %expert.3 = bf16[384,56,128]{2,1,0:T(8,128)(2,1)} custom-call(bf16[384,56,128]{2,1,0:T(8,128)(2,1)} %all-to-all-done.2.rec_in, bf16[3584,1024]{1,0:T(8,128)(2,1)} %bitcast.25, bf16[3584,1024]{1,0:T(8,128)(2,1)} %bitcast.27, bf16[1024,3584]{1,0:T(8,128)(2,1)} %bitcast.29), custom_call_target="tpu_custom_call" | custom-call | flops 16911433728 | bytes 33030144 | tf_op jit(solution)/shard_map/expert/pallas_call | solution.py:233
  120.4 15.3 %all-to-all-done.rec_in = bf16[256,56,128]{2,1,0:T(8,128)(2,1)} async-done(((bf16[256,56,128]{2,1,0:T(8,128)(2,1)}), bf16[256,56,128]{2,1,0:T(8,128)(2,1)}, u32[]{:S(2)}, u32[]{:S(2)}) %all-to-all-start) | async-done | bytes 3670048 | tf_op jit(solution)/shard_map/all_to_all | solution.py:400
  135.7 7.8 %all-to-all-start.3 = ((bf16[384,56,128]{2,1,0:T(8,128)(2,1)}), bf16[384,56,128]{2,1,0:T(8,128)(2,1)}, u32[]{:S(2)}, u32[]{:S(2)}) async-start(bf16[384,56,128]{2,1,0:T(8,128)(2,1)} %expert.3), calls=%async_computation.3 | async-start | bytes 11010048 | tf_op jit(solution)/shard_map/all_to_all | solution.py:400
  143.5 22.4 %expert.2 = bf16[256,56,128]{2,1,0:T(8,128)(2,1)} custom-call(bf16[256,56,128]{2,1,0:T(8,128)(2,1)} %all-to-all-done.rec_in, bf16[3584,1024]{1,0:T(8,128)(2,1)} %bitcast.26, bf16[3584,1024]{1,0:T(8,128)(2,1)} %bitcast.28, bf16[1024,3584]{1,0:T(8,128)(2,1)} %bitcast.30), custom_call_target="tpu_custom_call" | custom-call | flops 11274289152 | bytes 29360128 | tf_op jit(solution)/shard_map/expert/pallas_call | solution.py:233
  165.9 44.3 %all-to-all-done.3.rec_in = bf16[384,56,128]{2,1,0:T(8,128)(2,1)} async-done(((bf16[384,56,128]{2,1,0:T(8,128)(2,1)}), bf16[384,56,128]{2,1,0:T(8,128)(2,1)}, u32[]{:S(2)}, u32[]{:S(2)}) %all-to-all-start.3) | async-done | bytes 5505056 | tf_op jit(solution)/shard_map/all_to_all | solution.py:400
  210.2 8.4 %all-to-all-start.1 = ((bf16[256,56,128]{2,1,0:T(8,128)(2,1)}), bf16[256,56,128]{2,1,0:T(8,128)(2,1)}, u32[]{:S(2)}, u32[]{:S(2)}) async-start(bf16[256,56,128]{2,1,0:T(8,128)(2,1)} %expert.2), calls=%async_computation.1 | async-start | bytes 7340032 | tf_op jit(solution)/shard_map/all_to_all | solution.py:400
  218.6 8.2 %unpack.2 = (f32[65,32,128]{2,1,0:T(8,128)}, f32[64,3584]{1,0:T(8,128)}, f32[64,3584]{1,0:T(8,128)}, f32[8,64]{1,0:T(8,128)}) custom-call(s32[8,128]{1,0:T(8,128)} %get-tuple-element.12.table.table_in, f32[8,64]{1,0:T(8,128)} %bitcast.22, bf16[384,56,128]{2,1,0:T(8,128)(2,1)} %all-to-all-done.3.rec_in, bf16[64,3584]{1,0:T(8,128)(2,1)} %bitcast.18), custom_call_target="tpu_custom_call" | custom-call | flops 22020096 | bytes 11010048 | tf_op jit(solution)/shard_map/unpack/pallas_call | solution.py:373
  226.8 36.7 %all-to-all-done.1.rec_in = bf16[256,56,128]{2,1,0:T(8,128)(2,1)} async-done(((bf16[256,56,128]{2,1,0:T(8,128)(2,1)}), bf16[256,56,128]{2,1,0:T(8,128)(2,1)}, u32[]{:S(2)}, u32[]{:S(2)}) %all-to-all-start.1) | async-done | bytes 3670048 | tf_op jit(solution)/shard_map/all_to_all | solution.py:400
  263.6 5.9 %unpack.3 = (bf16[64,3584]{1,0:T(8,128)(2,1)}, bf16[64,3584]{1,0:T(8,128)(2,1)}, f32[8,64]{1,0:T(8,128)}) custom-call(s32[8,128]{1,0:T(8,128)} %get-tuple-element.12.table.table_in, f32[8,64]{1,0:T(8,128)} %bitcast.23, bf16[256,56,128]{2,1,0:T(8,128)(2,1)} %all-to-all-done.1.rec_in, bf16[64,3584]{1,0:T(8,128)(2,1)} %bitcast.19, ...), custom_call_target="tpu_custom_call" | custom-call | flops 14680064 | bytes 7340032 | tf_op jit(solution)/shard_map/unpack/pallas_call | solution.py:373
Async XLA Ops:
  5.0 77.4 %all-to-all-start.2 = ((bf16[384,56,128]{2,1,0:T(8,128)(2,1)}), bf16[384,56,128]{2,1,0:T(8,128)(2,1)}, u32[]{:S(2)}, u32[]{:S(2)}) async-start(bf16[384,56,128]{2,1,0:T(8,128)(2,1)} %get-tuple-element.13), calls=%async_computation.2 | async-start | bytes 11010048 | tf_op jit(solution)/shard_map/all_to_all | solution.py:400
  82.4 53.4 %all-to-all-start = ((bf16[256,56,128]{2,1,0:T(8,128)(2,1)}), bf16[256,56,128]{2,1,0:T(8,128)(2,1)}, u32[]{:S(2)}, u32[]{:S(2)}) async-start(bf16[256,56,128]{2,1,0:T(8,128)(2,1)} %next_pack.1), calls=%async_computation | async-start | bytes 7340032 | tf_op jit(solution)/shard_map/all_to_all | solution.py:400
  135.7 74.5 %all-to-all-start.3 = ((bf16[384,56,128]{2,1,0:T(8,128)(2,1)}), bf16[384,56,128]{2,1,0:T(8,128)(2,1)}, u32[]{:S(2)}, u32[]{:S(2)}) async-start(bf16[384,56,128]{2,1,0:T(8,128)(2,1)} %expert.3), calls=%async_computation.3 | async-start | bytes 11010048 | tf_op jit(solution)/shard_map/all_to_all | solution.py:400
  210.2 53.3 %all-to-all-start.1 = ((bf16[256,56,128]{2,1,0:T(8,128)(2,1)}), bf16[256,56,128]{2,1,0:T(8,128)(2,1)}, u32[]{:S(2)}, u32[]{:S(2)}) async-start(bf16[256,56,128]{2,1,0:T(8,128)(2,1)} %expert.2), calls=%async_computation.1 | async-start | bytes 7340032 | tf_op jit(solution)/shard_map/all_to_all | solution.py:400
